TPU v7x, 256 devices: a whole 4x4x8 slice. The times are simulated.
256 devices in a mesh: seq: 32 (over y, z), expert: 8 (over x, core).
Axes of the slice: x: 4, y: 4, z: 8, core: 2. Of those that a mesh axis runs over, the one named last changes fastest.
Arguments:
- grad_out: bfloat16 [32768, 2048], P(('seq', 'expert')), may hold values from -6 to 6
- expert_input: bfloat16 [32768, 2048], P(('seq', 'expert')), may hold values from -6 to 6
- expert_index: int32 [32768, 2], P(('seq', 'expert')), may hold values from 0 to 7, all different within a row; in each aligned block of 128 rows (0 to 127, 128 to 255, ...) at most 64 rows name the same one
- route_weight: float32 [32768, 2], P(('seq', 'expert')), may hold values from 0.1 to 1
- up_weight: bfloat16 [8, 2048, 768], P('expert'), may hold values from -0.125 to 0.125
- down_weight: bfloat16 [8, 768, 2048], P('expert'), may hold values from -0.21875 to 0.21875
- out_weight: bfloat16 [4096, 2048], P('expert'), may hold values from -0.125 to 0.125
- conv_value: bfloat16 [32768, 4096], P('seq', 'expert'), may hold values from -6 to 6
- conv_weight: float32 [4, 4096], P(None, 'expert'), may hold values from -3 to 3
- step_size: float32 [64, 32768], P('expert', 'seq'), may hold values from 0.25 to 1
- log_decay: float32 [64, 32768], P('expert', 'seq'), may hold values from -1 to 0
- skip_gain: float32 [64], P('expert'), may hold values from 0.2 to 0.6
- input_basis: bfloat16 [32768, 1024], P('seq', 'expert'), may hold values from -0.09375 to 0.09375
- output_basis: bfloat16 [32768, 1024], P('seq', 'expert'), may hold values from -0.09375 to 0.09375
Outputs:
- residual_grad: bfloat16 [32768, 2048], P(('seq', 'expert'))
- conv_grad: bfloat16 [32768, 4096], P('seq', 'expert')
- input_basis_grad: bfloat16 [32768, 1024], P('seq', 'expert')
- output_basis_grad: bfloat16 [32768, 1024], P('seq', 'expert')
Inputs may be any that keep to these rules, and one draw needn't show every extreme that they name: `expert_index`: in each aligned block of 128 rows (the rows of one device), no expert is named by more than 64 rows, and the 2 experts of a row differ.
All inputs are finite; a program needn't handle non-finite values.
Results may differ from a plain program's by a relative error of at most 0.01.
Values may be sent and summed in bfloat16 or wider, within the bound.
A program may use at most 128 MiB of HBM per device.

v0:
```python
import jax
import jax.numpy as jnp
from jax import lax
from jax.sharding import PartitionSpec as P

P_SIZE = 64
N = 128
KW = 4
SPAN = 128


def from_behind(value, axis, by):
    devices = lax.axis_size(axis)
    pairs = [(i, i + by) for i in range(devices) if 0 <= i + by < devices]
    return lax.ppermute(value, axis, pairs)


def slot_tables(block_index, block_weight, expert_count, capacity):
    flat_index = block_index.reshape(-1)
    onehot_table = (
        flat_index[:, None] == jnp.arange(expert_count, dtype=jnp.int32)[None, :]
    ).astype(jnp.int32)
    earlier_count = jnp.cumsum(onehot_table, axis=0) - onehot_table
    slot_rank = jnp.sum(earlier_count * onehot_table, axis=1)
    slot_place = flat_index * capacity + slot_rank
    owner_row = jnp.arange(flat_index.shape[0], dtype=jnp.int32) // block_index.shape[1]
    slot_match = (
        slot_place[:, None] == jnp.arange(expert_count * capacity, dtype=jnp.int32)[None, :]
    )
    source_row = jnp.sum(jnp.where(slot_match, owner_row[:, None], 0), axis=0)
    slot_filled = jnp.any(slot_match, axis=0)
    slot_weight = jnp.sum(jnp.where(slot_match, block_weight.reshape(-1)[:, None], 0.0), axis=0)
    return (slot_place, source_row, slot_filled, slot_weight)


def expert_rows(input_rows, grad_rows, up_matrix, down_matrix):
    hidden_pre = jnp.dot(input_rows, up_matrix, preferred_element_type=jnp.float32)
    hidden_back = jnp.dot(grad_rows, down_matrix.T, preferred_element_type=jnp.float32)
    inner_grad = (2.0 * jnp.maximum(hidden_pre, 0.0) * hidden_back).astype(jnp.bfloat16)
    return jnp.dot(inner_grad, up_matrix.T, preferred_element_type=jnp.float32).astype(jnp.bfloat16)


def combine_rows(grad_rows, slot_place, returned):
    row_count = grad_rows.shape[0]
    flat_rows = returned.reshape(-1, returned.shape[-1])
    picked = (
        jnp.take(flat_rows, slot_place, axis=0)
        .astype(jnp.float32)
        .reshape(row_count, -1, flat_rows.shape[-1])
    )
    return (grad_rows.astype(jnp.float32) + jnp.sum(picked, axis=1)).astype(jnp.bfloat16)


def silu_grad(values):
    sigmoid_value = jax.nn.sigmoid(values)
    return sigmoid_value + values * sigmoid_value * (1.0 - sigmoid_value)


def forward_terms(mixed_act, in_basis, step_blocks, decay_blocks):
    cumulative = jnp.cumsum(decay_blocks, axis=-1)
    in_scale = jnp.exp(cumulative[..., -1:] - cumulative) * step_blocks
    row_scale = jnp.transpose(in_scale, (2, 3, 0, 1))[..., None]
    mixed_weighted = (mixed_act.astype(jnp.float32) * row_scale).astype(jnp.bfloat16)
    local_end = jnp.einsum(
        "kqgn,kqghp->ghknp", in_basis, mixed_weighted, preferred_element_type=jnp.float32
    )
    return (cumulative, in_scale, mixed_weighted, local_end, jnp.exp(cumulative[..., -1]))


def backward_terms(cumulative, out_grad, out_basis):
    row_scale = jnp.transpose(jnp.exp(cumulative), (2, 3, 0, 1))[..., None]
    grad_weighted = (out_grad.astype(jnp.float32) * row_scale).astype(jnp.bfloat16)
    local_start = jnp.einsum(
        "kqgn,kqghp->ghknp", out_basis, grad_weighted, preferred_element_type=jnp.float32
    )
    return (grad_weighted, local_start)


def advance(state_now, pair_now):
    return (pair_now[0][..., None, None] * state_now + pair_now[1], state_now)


def chain_forward(block_decay, local_terms, initial):
    moved = (jnp.moveaxis(block_decay, 2, 0), jnp.moveaxis(local_terms, 2, 0))
    final, entering = lax.scan(advance, initial, moved)
    return (final, jnp.moveaxis(entering, 0, 2))


def chain_backward(block_decay, local_terms, initial):
    moved = (jnp.moveaxis(block_decay, 2, 0), jnp.moveaxis(local_terms, 2, 0))
    final, leaving = lax.scan(advance, initial, moved, reverse=True)
    return (final, jnp.moveaxis(leaving, 0, 2))


def block_grads(
    cumulative,
    in_scale,
    mixed_act,
    out_grad,
    in_basis,
    out_basis,
    mixed_weighted,
    grad_weighted,
    entering,
    leaving,
    step_blocks,
    skip_heads,
):
    block_len = cumulative.shape[-1]
    lower_mask = jnp.arange(block_len)[:, None] >= jnp.arange(block_len)[None, :]
    spread = jnp.where(lower_mask, cumulative[..., :, None] - cumulative[..., None, :], 0.0)
    decay_mask = jnp.where(lower_mask, jnp.exp(spread), 0.0)
    step_column = step_blocks[..., None, :]
    scores = jnp.einsum("kagn,kbgn->gkab", out_basis, in_basis, preferred_element_type=jnp.float32)
    weight_scores = (decay_mask * step_column * scores[:, None]).astype(jnp.bfloat16)
    grad_mixed = jnp.einsum(
        "kaghp,kbghp->ghkab", out_grad, mixed_act, preferred_element_type=jnp.float32
    )
    weight_grad = (decay_mask * step_column * grad_mixed).astype(jnp.bfloat16)
    entering_low = entering.astype(jnp.bfloat16)
    leaving_low = leaving.astype(jnp.bfloat16)
    inner_term = jnp.einsum(
        "ghkab,kaghp->kbghp", weight_scores, out_grad, preferred_element_type=jnp.float32
    )
    carried = jnp.einsum(
        "kbgn,ghknp->kbghp", in_basis, leaving_low, preferred_element_type=jnp.float32
    )
    row_scale = jnp.transpose(in_scale, (2, 3, 0, 1))[..., None]
    mixed_grad = (
        inner_term
        + row_scale * carried
        + skip_heads[None, None, :, :, None] * out_grad.astype(jnp.float32)
    )
    in_basis_grad = jnp.einsum(
        "ghkab,kagn->kbgn", weight_grad, out_basis, preferred_element_type=jnp.float32
    )
    in_basis_grad = in_basis_grad + jnp.einsum(
        "kbghp,ghknp->kbgn", mixed_weighted, leaving_low, preferred_element_type=jnp.float32
    )
    out_basis_grad = jnp.einsum(
        "kaghp,ghknp->kagn", grad_weighted, entering_low, preferred_element_type=jnp.float32
    )
    out_basis_grad = out_basis_grad + jnp.einsum(
        "ghkab,kbgn->kagn", weight_grad, in_basis, preferred_element_type=jnp.float32
    )
    return (mixed_grad, in_basis_grad, out_basis_grad)


def filter_back(value_grad, filter_taps, after_rows):
    row_count = value_grad.shape[0]
    padded = jnp.concatenate([value_grad, after_rows], axis=0)
    summed = filter_taps[0] * value_grad
    for tap_index in range(1, filter_taps.shape[0]):
        summed = summed + filter_taps[tap_index] * padded[tap_index : tap_index + row_count]
    return summed


def shards(
    grad_out,
    expert_input,
    expert_index,
    route_weight,
    up_weight,
    down_weight,
    out_weight,
    conv_value,
    conv_weight,
    step_size,
    log_decay,
    skip_gain,
    input_basis,
    output_basis,
):
    expert_count = lax.axis_size("expert")
    row_count, choose_count = expert_index.shape
    capacity = 2 * row_count * choose_count // expert_count
    model_width = grad_out.shape[1]
    head_count, seq_length = step_size.shape
    group_count = input_basis.shape[1] // N
    per_group = head_count // group_count
    block_count = seq_length // SPAN
    pre_value = conv_value.astype(jnp.float32)
    mixed_act = (
        jax.nn.silu(pre_value)
        .astype(jnp.bfloat16)
        .reshape(block_count, SPAN, group_count, per_group, P_SIZE)
    )
    in_basis = input_basis.reshape(block_count, SPAN, group_count, N)
    out_basis = output_basis.reshape(block_count, SPAN, group_count, N)
    step_blocks = step_size.reshape(group_count, per_group, block_count, SPAN)
    decay_blocks = log_decay.reshape(group_count, per_group, block_count, SPAN)
    skip_heads = skip_gain.reshape(group_count, per_group)
    cumulative, in_scale, mixed_weighted, local_end, block_decay = forward_terms(
        mixed_act, in_basis, step_blocks, decay_blocks
    )
    zero_state = jnp.zeros((group_count, per_group, N, P_SIZE), jnp.float32)
    device_decay = jnp.exp(jnp.sum(cumulative[..., -1], axis=-1))
    device_state, _ = chain_forward(block_decay, local_end, zero_state)

    def forward_turn(turn_index, incoming):
        return from_behind(
            (device_decay[..., None, None] * incoming + device_state).astype(jnp.bfloat16), "seq", 1
        ).astype(jnp.float32)

    enter_state = lax.fori_loop(0, lax.axis_size("seq") - 1, forward_turn, zero_state)
    _, entering = chain_forward(block_decay, local_end, enter_state)
    slot_place, source_row, slot_filled, slot_weight = slot_tables(
        expert_index, route_weight, expert_count, capacity
    )
    send_inputs = jnp.where(
        slot_filled[:, None],
        jnp.take(expert_input, source_row, axis=0),
        jnp.zeros((), expert_input.dtype),
    )
    send_grads = (
        jnp.take(grad_out, source_row, axis=0).astype(jnp.float32) * slot_weight[:, None]
    ).astype(jnp.bfloat16)
    send_inputs = send_inputs.reshape(expert_count, capacity, model_width)
    send_grads = send_grads.reshape(expert_count, capacity, model_width)
    up_local = up_weight[0]
    down_local = down_weight[0]
    arrived = (
        lax.all_to_all(send_inputs, "expert", split_axis=0, concat_axis=0, tiled=True),
        lax.all_to_all(send_grads, "expert", split_axis=0, concat_axis=0, tiled=True),
    )
    sender_count = arrived[0].shape[0]
    item_count = arrived[0].shape[1]
    result = expert_rows(
        arrived[0].reshape(sender_count * item_count, model_width),
        arrived[1].reshape(sender_count * item_count, model_width),
        up_local,
        down_local,
    )
    returned = lax.all_to_all(
        result.reshape(sender_count, item_count, model_width),
        "expert",
        split_axis=0,
        concat_axis=0,
        tiled=True,
    )
    residual_grad = combine_rows(grad_out, slot_place, returned)
    grad_rows = jnp.dot(
        lax.all_gather(residual_grad, "expert", axis=0, tiled=True),
        out_weight.T,
        preferred_element_type=jnp.float32,
    )
    out_grad = grad_rows.astype(jnp.bfloat16).reshape(
        block_count, SPAN, group_count, per_group, P_SIZE
    )
    grad_weighted, local_start = backward_terms(cumulative, out_grad, out_basis)
    device_grad, _ = chain_backward(block_decay, local_start, zero_state)

    def backward_turn(turn_index, incoming):
        return from_behind(
            (device_decay[..., None, None] * incoming + device_grad).astype(jnp.bfloat16), "seq", -1
        ).astype(jnp.float32)

    leave_grad = lax.fori_loop(0, lax.axis_size("seq") - 1, backward_turn, zero_state)
    _, leaving = chain_backward(block_decay, local_start, leave_grad)
    mixed_grad, in_grad, out_part = block_grads(
        cumulative,
        in_scale,
        mixed_act,
        out_grad,
        in_basis,
        out_basis,
        mixed_weighted,
        grad_weighted,
        entering,
        leaving,
        step_blocks,
        skip_heads,
    )
    value_grad = mixed_grad.reshape(seq_length, head_count * P_SIZE) * silu_grad(pre_value)
    after_rows = from_behind(value_grad[: KW - 1], "seq", -1)
    conv_grad = filter_back(value_grad, conv_weight, after_rows).astype(jnp.bfloat16)
    input_basis_grad = in_grad.reshape(seq_length, group_count * N).astype(jnp.bfloat16)
    output_basis_grad = out_part.reshape(seq_length, group_count * N).astype(jnp.bfloat16)
    return (residual_grad, conv_grad, input_basis_grad, output_basis_grad)


def solution(mesh):
    in_specs = (
        P(("seq", "expert"), None),
        P(("seq", "expert"), None),
        P(("seq", "expert"), None),
        P(("seq", "expert"), None),
        P("expert", None, None),
        P("expert", None, None),
        P("expert", None),
        P("seq", "expert"),
        P(None, "expert"),
        P("expert", "seq"),
        P("expert", "seq"),
        P("expert"),
        P("seq", "expert"),
        P("seq", "expert"),
    )
    out_specs = (
        P(("seq", "expert"), None),
        P("seq", "expert"),
        P("seq", "expert"),
        P("seq", "expert"),
    )
    return jax.shard_map(shards, mesh=mesh, in_specs=in_specs, out_specs=out_specs, check_vma=False)
```

profile of v0, /device:TPU:24, one launch (start us, length us, event | category | flops | bytes accessed | tf_op | source)
XLA Modules:
  0.0 1003.8 jit_solution(10444084823362101818)
XLA Ops:
  34.6 17.5 %all-to-all-done.1 = bf16[8,64,2048]{2,1,0:T(8,128)(2,1)} async-done(((bf16[8,64,2048]{2,1,0:T(8,128)(2,1)}), bf16[8,64,2048]{2,1,0:T(8,128)(2,1)}, u32[]{:S(2)}, u32[]{:S(2)}) %all-to-all-start.1) | async-done | bytes 2097184 | tf_op jit(solution)/shard_map/all_to_all | solution.py:224
  61.9 21.7 %all-to-all-done = bf16[8,64,2048]{2,1,0:T(8,128)(2,1)} async-done(((bf16[8,64,2048]{2,1,0:T(8,128)(2,1)}), bf16[8,64,2048]{2,1,0:T(8,128)(2,1)}, u32[]{:S(2)}, u32[]{:S(2)}) %all-to-all-start) | async-done | bytes 2097184 | tf_op jit(solution)/shard_map/all_to_all | solution.py:223
  95.6 26.2 %all-to-all-done.2 = bf16[8,64,2048]{2,1,0:T(8,128)(2,1)S(1)} async-done(((bf16[8,64,2048]{2,1,0:T(8,128)(2,1)}), bf16[8,64,2048]{2,1,0:T(8,128)(2,1)S(1)}, u32[]{:S(2)}, u32[]{:S(2)}) %all-to-all-start.2) | async-done | bytes 2097184 | tf_op jit(solution)/shard_map/all_to_all | solution.py:234
  137.3 27.1 %all-gather.2.cloned.1.call-done = bf16[1024,2048]{1,0:T(8,128)(2,1)} async-done(((bf16[128,2048]{1,0:T(8,128)(2,1)}), bf16[1024,2048]{1,0:T(8,128)(2,1)}) %all-gather.2.cloned.1.call-update) | async-done | bytes 4194320 | tf_op jit(solution)/shard_map/all_gather | solution.py:243
  181.7 14.6 %while.78 = (s32[]{:T(128)}, f32[1,8,128,64]{3,2,1,0:T(8,128)S(1)}, f32[8,1,8]{2,1,0:T(1,128)}, f32[8,1,8,128,64]{4,3,2,1,0:T(8,128)}, s32[]{:T(128)}, /*index=5*/s32[]{:T(128)}, s32[]{:T(128)}) while((s32[]{:T(128)}, f32[1,8,128,64]{3,2,1,0:T(8,128)S(1)}, f32[8,1,8]{2,1,0:T(1,128)}, f32[8,1,8,128,64]{4,3,2,1,0:T(8,128)}, ...), condition=%wide.region_10.12_spmd.clone, body=%wide.region_9.11_spmd.clone.sunk | while | flops 196612 | bytes 786643 | solution.py:91
  196.3 351.1 %while.79 = (s32[]{:T(128)}, f32[1,8,128,64]{3,2,1,0:T(8,128)S(1)}, f32[1,8]{1,0:T(1,128)S(1)}, f32[1,8,128,64]{3,2,1,0:T(8,128)S(1)}, s32[]{:T(128)}, /*index=5*/s32[]{:T(128)}) while((s32[]{:T(128)}, f32[1,8,128,64]{3,2,1,0:T(8,128)S(1)}, f32[1,8]{1,0:T(1,128)S(1)}, f32[1,8,128,64]{3,2,1,0:T(8,128)S(1)}, s32[]{:T(128)}, ...), condition=%wide.region_12.14_spmd.clone, body=%wide.region_11.13_spmd.clone.sunk | while | flops 327683 | bytes 1573015 | solution.py:258
  549.2 20.8 %while.76 = (s32[]{:T(128)}, f32[1,8,128,64]{3,2,1,0:T(8,128)S(1)}, bf16[8,1,8,128,64]{4,3,2,1,0:T(8,128)(2,1)}, f32[8,1,8]{2,1,0:T(1,128)}, f32[8,1,8,128,64]{4,3,2,1,0:T(8,128)}, /*index=5*/s32[]{:T(128)}, s32[]{:T(128)}) while((s32[]{:T(128)}, f32[1,8,128,64]{3,2,1,0:T(8,128)S(1)}, bf16[8,1,8,128,64]{4,3,2,1,0:T(8,128)(2,1)}, ...), condition=%wide.region_14.16_spmd, body=%wide.region_13.15_spmd.sunk | while | flops 131075 | bytes 1573069 | solution.py:91
  598.0 14.6 %while.80 = (s32[]{:T(128)}, f32[1,8,128,64]{3,2,1,0:T(8,128)S(1)}, f32[8,1,8]{2,1,0:T(1,128)}, f32[8,1,8,128,64]{4,3,2,1,0:T(8,128)}, s32[]{:T(128)}, /*index=5*/s32[]{:T(128)}) while((s32[]{:T(128)}, f32[1,8,128,64]{3,2,1,0:T(8,128)S(1)}, f32[8,1,8]{2,1,0:T(1,128)}, f32[8,1,8,128,64]{4,3,2,1,0:T(8,128)}, s32[]{:T(128)}, ...), condition=%wide.region_17.19_spmd.clone, body=%wide.region_16.18_spmd.clone.sunk | while | flops 196611 | bytes 786623 | solution.py:85
  612.6 349.9 %while.81 = (s32[]{:T(128)}, f32[1,8,128,64]{3,2,1,0:T(8,128)S(1)}, f32[1,8]{1,0:T(1,128)S(1)}, f32[1,8,128,64]{3,2,1,0:T(8,128)S(1)}, s32[]{:T(128)}, /*index=5*/s32[]{:T(128)}) while((s32[]{:T(128)}, f32[1,8,128,64]{3,2,1,0:T(8,128)S(1)}, f32[1,8]{1,0:T(1,128)S(1)}, f32[1,8,128,64]{3,2,1,0:T(8,128)S(1)}, s32[]{:T(128)}, ...), condition=%wide.region_19.21_spmd.clone, body=%wide.region_18.20_spmd.clone.sunk | while | flops 327683 | bytes 1573015 | solution.py:205
  614.7 8.4 collective-permute-done.1
  625.2 8.4 collective-permute-done.1
  635.8 9.5 collective-permute-done.1
  647.4 10.7 %collective-permute-done.1 = bf16[1,8,128,64]{3,2,1,0:T(8,128)(2,1)S(1)} collective-permute-done((bf16[1,8,128,64]{3,2,1,0:T(8,128)(2,1)S(1)}, bf16[1,8,128,64]{3,2,1,0:T(8,128)(2,1)S(1)}, u32[]{:S(2)}, u32[]{:S(2)}) %collective-permute-start.1) | collective-permute-done | bytes 131104 | tf_op jit(solution)/shard_map/while/body/eval_jaxpr/ppermute | solution.py:15
  660.2 10.7 %collective-permute-done.1 = bf16[1,8,128,64]{3,2,1,0:T(8,128)(2,1)S(1)} collective-permute-done((bf16[1,8,128,64]{3,2,1,0:T(8,128)(2,1)S(1)}, bf16[1,8,128,64]{3,2,1,0:T(8,128)(2,1)S(1)}, u32[]{:S(2)}, u32[]{:S(2)}) %collective-permute-start.1) | collective-permute-done | bytes 131104 | tf_op jit(solution)/shard_map/while/body/eval_jaxpr/ppermute | solution.py:15
  673.0 9.9 collective-permute-done.1
  685.1 9.0 collective-permute-done.1
  696.2 8.4 collective-permute-done.1
  706.8 8.4 collective-permute-done.1
  717.3 8.4 collective-permute-done.1
  727.9 8.4 collective-permute-done.1
  738.5 9.5 collective-permute-done.1
  750.1 10.7 %collective-permute-done.1 = bf16[1,8,128,64]{3,2,1,0:T(8,128)(2,1)S(1)} collective-permute-done((bf16[1,8,128,64]{3,2,1,0:T(8,128)(2,1)S(1)}, bf16[1,8,128,64]{3,2,1,0:T(8,128)(2,1)S(1)}, u32[]{:S(2)}, u32[]{:S(2)}) %collective-permute-start.1) | collective-permute-done | bytes 131104 | tf_op jit(solution)/shard_map/while/body/eval_jaxpr/ppermute | solution.py:15
  762.9 10.6 %collective-permute-done.1 = bf16[1,8,128,64]{3,2,1,0:T(8,128)(2,1)S(1)} collective-permute-done((bf16[1,8,128,64]{3,2,1,0:T(8,128)(2,1)S(1)}, bf16[1,8,128,64]{3,2,1,0:T(8,128)(2,1)S(1)}, u32[]{:S(2)}, u32[]{:S(2)}) %collective-permute-start.1) | collective-permute-done | bytes 131104 | tf_op jit(solution)/shard_map/while/body/eval_jaxpr/ppermute | solution.py:15
  775.7 9.8 collective-permute-done.1
  787.7 8.9 collective-permute-done.1
  830.4 8.5 collective-permute-done.1
  841.0 9.5 collective-permute-done.1
  852.7 10.8 %collective-permute-done.1 = bf16[1,8,128,64]{3,2,1,0:T(8,128)(2,1)S(1)} collective-permute-done((bf16[1,8,128,64]{3,2,1,0:T(8,128)(2,1)S(1)}, bf16[1,8,128,64]{3,2,1,0:T(8,128)(2,1)S(1)}, u32[]{:S(2)}, u32[]{:S(2)}) %collective-permute-start.1) | collective-permute-done | bytes 131104 | tf_op jit(solution)/shard_map/while/body/eval_jaxpr/ppermute | solution.py:15
  865.5 10.6 %collective-permute-done.1 = bf16[1,8,128,64]{3,2,1,0:T(8,128)(2,1)S(1)} collective-permute-done((bf16[1,8,128,64]{3,2,1,0:T(8,128)(2,1)S(1)}, bf16[1,8,128,64]{3,2,1,0:T(8,128)(2,1)S(1)}, u32[]{:S(2)}, u32[]{:S(2)}) %collective-permute-start.1) | collective-permute-done | bytes 131104 | tf_op jit(solution)/shard_map/while/body/eval_jaxpr/ppermute | solution.py:15
  878.3 9.8 collective-permute-done.1
  890.2 8.9 collective-permute-done.1
  964.3 20.7 %while.77 = (s32[]{:T(128)}, f32[1,8,128,64]{3,2,1,0:T(8,128)S(1)}, bf16[8,1,8,128,64]{4,3,2,1,0:T(8,128)(2,1)}, f32[8,1,8]{2,1,0:T(1,128)}, f32[8,1,8,128,64]{4,3,2,1,0:T(8,128)}, /*index=5*/s32[]{:T(128)}) while((s32[]{:T(128)}, f32[1,8,128,64]{3,2,1,0:T(8,128)S(1)}, bf16[8,1,8,128,64]{4,3,2,1,0:T(8,128)(2,1)}, f32[8,1,8]{2,1,0:T(1,128)}, ...), condition=%wide.region_21.23_spmd, body=%wide.region_20.22_spmd.sunk | while | flops 131074 | bytes 1573049 | solution.py:85
  (448 shorter events, 686.0 us)
Async XLA Ops:
  20.5 31.6 %all-to-all-start.1 = ((bf16[8,64,2048]{2,1,0:T(8,128)(2,1)}), bf16[8,64,2048]{2,1,0:T(8,128)(2,1)}, u32[]{:S(2)}, u32[]{:S(2)}) async-start(bf16[8,64,2048]{2,1,0:T(8,128)(2,1)} %bitcast.209), calls=%async_computation.1 | async-start | bytes 4194304 | tf_op jit(solution)/shard_map/all_to_all | solution.py:224
  52.1 31.5 %all-to-all-start = ((bf16[8,64,2048]{2,1,0:T(8,128)(2,1)}), bf16[8,64,2048]{2,1,0:T(8,128)(2,1)}, u32[]{:S(2)}, u32[]{:S(2)}) async-start(bf16[8,64,2048]{2,1,0:T(8,128)(2,1)} %bitcast.208), calls=%async_computation | async-start | bytes 4194304 | tf_op jit(solution)/shard_map/all_to_all | solution.py:223
  90.9 30.9 %all-to-all-start.2 = ((bf16[8,64,2048]{2,1,0:T(8,128)(2,1)}), bf16[8,64,2048]{2,1,0:T(8,128)(2,1)S(1)}, u32[]{:S(2)}, u32[]{:S(2)}) async-start(bf16[8,64,2048]{2,1,0:T(8,128)(2,1)} %bitcast.223), calls=%async_computation.2 | async-start | bytes 4194304 | tf_op jit(solution)/shard_map/all_to_all | solution.py:234
  94.7 69.7 %all-gather.2.cloned.1.call-start = ((), (), s32[]{:S(2)}) async-start(), calls=%async_computation.3 | async-start | bytes 4718592 | tf_op jit(solution)/shard_map/all_gather | solution.py:243
  196.4 11.5 %collective-permute-start = (bf16[1,8,128,64]{3,2,1,0:T(8,128)(2,1)S(1)}, bf16[1,8,128,64]{3,2,1,0:T(8,128)(2,1)S(1)}, u32[]{:S(2)}, u32[]{:S(2)}) collective-permute-start(bf16[1,8,128,64]{3,2,1,0:T(8,128)(2,1)S(1)} %fusion.99), channel_id=1, source_target_pairs={{8,0},{16,8},{24,16},{32,24},{40,32},{48,40},{56,48},{64,56},{72,6... | collective-permute-start | bytes 393224 | tf_op jit(solution)/shard_map/while/body/eval_jaxpr/ppermute | solution.py:15
  208.1 11.7 %collective-permute-start = (bf16[1,8,128,64]{3,2,1,0:T(8,128)(2,1)S(1)}, bf16[1,8,128,64]{3,2,1,0:T(8,128)(2,1)S(1)}, u32[]{:S(2)}, u32[]{:S(2)}) collective-permute-start(bf16[1,8,128,64]{3,2,1,0:T(8,128)(2,1)S(1)} %fusion.99), channel_id=1, source_target_pairs={{8,0},{16,8},{24,16},{32,24},{40,32},{48,40},{56,48},{64,56},{72,6... | collective-permute-start | bytes 393224 | tf_op jit(solution)/shard_map/while/body/eval_jaxpr/ppermute | solution.py:15
  273.3 11.6 %collective-permute-start = (bf16[1,8,128,64]{3,2,1,0:T(8,128)(2,1)S(1)}, bf16[1,8,128,64]{3,2,1,0:T(8,128)(2,1)S(1)}, u32[]{:S(2)}, u32[]{:S(2)}) collective-permute-start(bf16[1,8,128,64]{3,2,1,0:T(8,128)(2,1)S(1)} %fusion.99), channel_id=1, source_target_pairs={{8,0},{16,8},{24,16},{32,24},{40,32},{48,40},{56,48},{64,56},{72,6... | collective-permute-start | bytes 393224 | tf_op jit(solution)/shard_map/while/body/eval_jaxpr/ppermute | solution.py:15
  285.1 12.8 %collective-permute-start = (bf16[1,8,128,64]{3,2,1,0:T(8,128)(2,1)S(1)}, bf16[1,8,128,64]{3,2,1,0:T(8,128)(2,1)S(1)}, u32[]{:S(2)}, u32[]{:S(2)}) collective-permute-start(bf16[1,8,128,64]{3,2,1,0:T(8,128)(2,1)S(1)} %fusion.99), channel_id=1, source_target_pairs={{8,0},{16,8},{24,16},{32,24},{40,32},{48,40},{56,48},{64,56},{72,6... | collective-permute-start | bytes 393224 | tf_op jit(solution)/shard_map/while/body/eval_jaxpr/ppermute | solution.py:15
  298.1 12.4 %collective-permute-start = (bf16[1,8,128,64]{3,2,1,0:T(8,128)(2,1)S(1)}, bf16[1,8,128,64]{3,2,1,0:T(8,128)(2,1)S(1)}, u32[]{:S(2)}, u32[]{:S(2)}) collective-permute-start(bf16[1,8,128,64]{3,2,1,0:T(8,128)(2,1)S(1)} %fusion.99), channel_id=1, source_target_pairs={{8,0},{16,8},{24,16},{32,24},{40,32},{48,40},{56,48},{64,56},{72,6... | collective-permute-start | bytes 393224 | tf_op jit(solution)/shard_map/while/body/eval_jaxpr/ppermute | solution.py:15
  310.7 11.6 %collective-permute-start = (bf16[1,8,128,64]{3,2,1,0:T(8,128)(2,1)S(1)}, bf16[1,8,128,64]{3,2,1,0:T(8,128)(2,1)S(1)}, u32[]{:S(2)}, u32[]{:S(2)}) collective-permute-start(bf16[1,8,128,64]{3,2,1,0:T(8,128)(2,1)S(1)} %fusion.99), channel_id=1, source_target_pairs={{8,0},{16,8},{24,16},{32,24},{40,32},{48,40},{56,48},{64,56},{72,6... | collective-permute-start | bytes 393224 | tf_op jit(solution)/shard_map/while/body/eval_jaxpr/ppermute | solution.py:15
  375.7 11.7 %collective-permute-start = (bf16[1,8,128,64]{3,2,1,0:T(8,128)(2,1)S(1)}, bf16[1,8,128,64]{3,2,1,0:T(8,128)(2,1)S(1)}, u32[]{:S(2)}, u32[]{:S(2)}) collective-permute-start(bf16[1,8,128,64]{3,2,1,0:T(8,128)(2,1)S(1)} %fusion.99), channel_id=1, source_target_pairs={{8,0},{16,8},{24,16},{32,24},{40,32},{48,40},{56,48},{64,56},{72,6... | collective-permute-start | bytes 393224 | tf_op jit(solution)/shard_map/while/body/eval_jaxpr/ppermute | solution.py:15
  387.6 12.8 %collective-permute-start = (bf16[1,8,128,64]{3,2,1,0:T(8,128)(2,1)S(1)}, bf16[1,8,128,64]{3,2,1,0:T(8,128)(2,1)S(1)}, u32[]{:S(2)}, u32[]{:S(2)}) collective-permute-start(bf16[1,8,128,64]{3,2,1,0:T(8,128)(2,1)S(1)} %fusion.99), channel_id=1, source_target_pairs={{8,0},{16,8},{24,16},{32,24},{40,32},{48,40},{56,48},{64,56},{72,6... | collective-permute-start | bytes 393224 | tf_op jit(solution)/shard_map/while/body/eval_jaxpr/ppermute | solution.py:15
  400.7 12.4 %collective-permute-start = (bf16[1,8,128,64]{3,2,1,0:T(8,128)(2,1)S(1)}, bf16[1,8,128,64]{3,2,1,0:T(8,128)(2,1)S(1)}, u32[]{:S(2)}, u32[]{:S(2)}) collective-permute-start(bf16[1,8,128,64]{3,2,1,0:T(8,128)(2,1)S(1)} %fusion.99), channel_id=1, source_target_pairs={{8,0},{16,8},{24,16},{32,24},{40,32},{48,40},{56,48},{64,56},{72,6... | collective-permute-start | bytes 393224 | tf_op jit(solution)/shard_map/while/body/eval_jaxpr/ppermute | solution.py:15
  413.2 11.5 %collective-permute-start = (bf16[1,8,128,64]{3,2,1,0:T(8,128)(2,1)S(1)}, bf16[1,8,128,64]{3,2,1,0:T(8,128)(2,1)S(1)}, u32[]{:S(2)}, u32[]{:S(2)}) collective-permute-start(bf16[1,8,128,64]{3,2,1,0:T(8,128)(2,1)S(1)} %fusion.99), channel_id=1, source_target_pairs={{8,0},{16,8},{24,16},{32,24},{40,32},{48,40},{56,48},{64,56},{72,6... | collective-permute-start | bytes 393224 | tf_op jit(solution)/shard_map/while/body/eval_jaxpr/ppermute | solution.py:15
  478.3 11.7 %collective-permute-start = (bf16[1,8,128,64]{3,2,1,0:T(8,128)(2,1)S(1)}, bf16[1,8,128,64]{3,2,1,0:T(8,128)(2,1)S(1)}, u32[]{:S(2)}, u32[]{:S(2)}) collective-permute-start(bf16[1,8,128,64]{3,2,1,0:T(8,128)(2,1)S(1)} %fusion.99), channel_id=1, source_target_pairs={{8,0},{16,8},{24,16},{32,24},{40,32},{48,40},{56,48},{64,56},{72,6... | collective-permute-start | bytes 393224 | tf_op jit(solution)/shard_map/while/body/eval_jaxpr/ppermute | solution.py:15
  490.2 12.9 %collective-permute-start = (bf16[1,8,128,64]{3,2,1,0:T(8,128)(2,1)S(1)}, bf16[1,8,128,64]{3,2,1,0:T(8,128)(2,1)S(1)}, u32[]{:S(2)}, u32[]{:S(2)}) collective-permute-start(bf16[1,8,128,64]{3,2,1,0:T(8,128)(2,1)S(1)} %fusion.99), channel_id=1, source_target_pairs={{8,0},{16,8},{24,16},{32,24},{40,32},{48,40},{56,48},{64,56},{72,6... | collective-permute-start | bytes 393224 | tf_op jit(solution)/shard_map/while/body/eval_jaxpr/ppermute | solution.py:15
  503.3 12.3 %collective-permute-start = (bf16[1,8,128,64]{3,2,1,0:T(8,128)(2,1)S(1)}, bf16[1,8,128,64]{3,2,1,0:T(8,128)(2,1)S(1)}, u32[]{:S(2)}, u32[]{:S(2)}) collective-permute-start(bf16[1,8,128,64]{3,2,1,0:T(8,128)(2,1)S(1)} %fusion.99), channel_id=1, source_target_pairs={{8,0},{16,8},{24,16},{32,24},{40,32},{48,40},{56,48},{64,56},{72,6... | collective-permute-start | bytes 393224 | tf_op jit(solution)/shard_map/while/body/eval_jaxpr/ppermute | solution.py:15
  587.7 401.9 %collective-permute-start.2 = (f32[3,512]{0,1:T(8,128)}, f32[3,512]{0,1:T(8,128)}, u32[]{:S(2)}, u32[]{:S(2)}) collective-permute-start(f32[3,512]{0,1:T(8,128)} %slice.54), channel_id=1, source_target_pairs={{8,0},{16,8},{24,16},{32,24},{40,32},{48,40},{56,48},{64,56},{72,6... | collective-permute-start | bytes 18440 | tf_op jit(solution)/shard_map/ppermute | solution.py:15
  633.9 11.4 %collective-permute-start.1 = (bf16[1,8,128,64]{3,2,1,0:T(8,128)(2,1)S(1)}, bf16[1,8,128,64]{3,2,1,0:T(8,128)(2,1)S(1)}, u32[]{:S(2)}, u32[]{:S(2)}) collective-permute-start(bf16[1,8,128,64]{3,2,1,0:T(8,128)(2,1)S(1)} %fusion.100), channel_id=1, source_target_pairs={{0,8},{8,16},{16,24},{24,32},{32,40},{40,48},{48,56},{56,64},{64,7... | collective-permute-start | bytes 393224 | tf_op jit(solution)/shard_map/while/body/eval_jaxpr/ppermute | solution.py:15
  645.5 12.6 %collective-permute-start.1 = (bf16[1,8,128,64]{3,2,1,0:T(8,128)(2,1)S(1)}, bf16[1,8,128,64]{3,2,1,0:T(8,128)(2,1)S(1)}, u32[]{:S(2)}, u32[]{:S(2)}) collective-permute-start(bf16[1,8,128,64]{3,2,1,0:T(8,128)(2,1)S(1)} %fusion.100), channel_id=1, source_target_pairs={{0,8},{8,16},{16,24},{24,32},{32,40},{40,48},{48,56},{56,64},{64,7... | collective-permute-start | bytes 393224 | tf_op jit(solution)/shard_map/while/body/eval_jaxpr/ppermute | solution.py:15
  658.2 12.6 %collective-permute-start.1 = (bf16[1,8,128,64]{3,2,1,0:T(8,128)(2,1)S(1)}, bf16[1,8,128,64]{3,2,1,0:T(8,128)(2,1)S(1)}, u32[]{:S(2)}, u32[]{:S(2)}) collective-permute-start(bf16[1,8,128,64]{3,2,1,0:T(8,128)(2,1)S(1)} %fusion.100), channel_id=1, source_target_pairs={{0,8},{8,16},{16,24},{24,32},{32,40},{40,48},{48,56},{56,64},{64,7... | collective-permute-start | bytes 393224 | tf_op jit(solution)/shard_map/while/body/eval_jaxpr/ppermute | solution.py:15
  671.1 11.9 %collective-permute-start.1 = (bf16[1,8,128,64]{3,2,1,0:T(8,128)(2,1)S(1)}, bf16[1,8,128,64]{3,2,1,0:T(8,128)(2,1)S(1)}, u32[]{:S(2)}, u32[]{:S(2)}) collective-permute-start(bf16[1,8,128,64]{3,2,1,0:T(8,128)(2,1)S(1)} %fusion.100), channel_id=1, source_target_pairs={{0,8},{8,16},{16,24},{24,32},{32,40},{40,48},{48,56},{56,64},{64,7... | collective-permute-start | bytes 393224 | tf_op jit(solution)/shard_map/while/body/eval_jaxpr/ppermute | solution.py:15
  683.1 11.0 %collective-permute-start.1 = (bf16[1,8,128,64]{3,2,1,0:T(8,128)(2,1)S(1)}, bf16[1,8,128,64]{3,2,1,0:T(8,128)(2,1)S(1)}, u32[]{:S(2)}, u32[]{:S(2)}) collective-permute-start(bf16[1,8,128,64]{3,2,1,0:T(8,128)(2,1)S(1)} %fusion.100), channel_id=1, source_target_pairs={{0,8},{8,16},{16,24},{24,32},{32,40},{40,48},{48,56},{56,64},{64,7... | collective-permute-start | bytes 393224 | tf_op jit(solution)/shard_map/while/body/eval_jaxpr/ppermute | solution.py:15
  736.5 11.4 %collective-permute-start.1 = (bf16[1,8,128,64]{3,2,1,0:T(8,128)(2,1)S(1)}, bf16[1,8,128,64]{3,2,1,0:T(8,128)(2,1)S(1)}, u32[]{:S(2)}, u32[]{:S(2)}) collective-permute-start(bf16[1,8,128,64]{3,2,1,0:T(8,128)(2,1)S(1)} %fusion.100), channel_id=1, source_target_pairs={{0,8},{8,16},{16,24},{24,32},{32,40},{40,48},{48,56},{56,64},{64,7... | collective-permute-start | bytes 393224 | tf_op jit(solution)/shard_map/while/body/eval_jaxpr/ppermute | solution.py:15
  748.2 12.7 %collective-permute-start.1 = (bf16[1,8,128,64]{3,2,1,0:T(8,128)(2,1)S(1)}, bf16[1,8,128,64]{3,2,1,0:T(8,128)(2,1)S(1)}, u32[]{:S(2)}, u32[]{:S(2)}) collective-permute-start(bf16[1,8,128,64]{3,2,1,0:T(8,128)(2,1)S(1)} %fusion.100), channel_id=1, source_target_pairs={{0,8},{8,16},{16,24},{24,32},{32,40},{40,48},{48,56},{56,64},{64,7... | collective-permute-start | bytes 393224 | tf_op jit(solution)/shard_map/while/body/eval_jaxpr/ppermute | solution.py:15
  761.0 12.6 %collective-permute-start.1 = (bf16[1,8,128,64]{3,2,1,0:T(8,128)(2,1)S(1)}, bf16[1,8,128,64]{3,2,1,0:T(8,128)(2,1)S(1)}, u32[]{:S(2)}, u32[]{:S(2)}) collective-permute-start(bf16[1,8,128,64]{3,2,1,0:T(8,128)(2,1)S(1)} %fusion.100), channel_id=1, source_target_pairs={{0,8},{8,16},{16,24},{24,32},{32,40},{40,48},{48,56},{56,64},{64,7... | collective-permute-start | bytes 393224 | tf_op jit(solution)/shard_map/while/body/eval_jaxpr/ppermute | solution.py:15
  773.8 11.8 %collective-permute-start.1 = (bf16[1,8,128,64]{3,2,1,0:T(8,128)(2,1)S(1)}, bf16[1,8,128,64]{3,2,1,0:T(8,128)(2,1)S(1)}, u32[]{:S(2)}, u32[]{:S(2)}) collective-permute-start(bf16[1,8,128,64]{3,2,1,0:T(8,128)(2,1)S(1)} %fusion.100), channel_id=1, source_target_pairs={{0,8},{8,16},{16,24},{24,32},{32,40},{40,48},{48,56},{56,64},{64,7... | collective-permute-start | bytes 393224 | tf_op jit(solution)/shard_map/while/body/eval_jaxpr/ppermute | solution.py:15
  785.7 10.9 %collective-permute-start.1 = (bf16[1,8,128,64]{3,2,1,0:T(8,128)(2,1)S(1)}, bf16[1,8,128,64]{3,2,1,0:T(8,128)(2,1)S(1)}, u32[]{:S(2)}, u32[]{:S(2)}) collective-permute-start(bf16[1,8,128,64]{3,2,1,0:T(8,128)(2,1)S(1)} %fusion.100), channel_id=1, source_target_pairs={{0,8},{8,16},{16,24},{24,32},{32,40},{40,48},{48,56},{56,64},{64,7... | collective-permute-start | bytes 393224 | tf_op jit(solution)/shard_map/while/body/eval_jaxpr/ppermute | solution.py:15
  839.1 11.5 %collective-permute-start.1 = (bf16[1,8,128,64]{3,2,1,0:T(8,128)(2,1)S(1)}, bf16[1,8,128,64]{3,2,1,0:T(8,128)(2,1)S(1)}, u32[]{:S(2)}, u32[]{:S(2)}) collective-permute-start(bf16[1,8,128,64]{3,2,1,0:T(8,128)(2,1)S(1)} %fusion.100), channel_id=1, source_target_pairs={{0,8},{8,16},{16,24},{24,32},{32,40},{40,48},{48,56},{56,64},{64,7... | collective-permute-start | bytes 393224 | tf_op jit(solution)/shard_map/while/body/eval_jaxpr/ppermute | solution.py:15
  850.7 12.7 %collective-permute-start.1 = (bf16[1,8,128,64]{3,2,1,0:T(8,128)(2,1)S(1)}, bf16[1,8,128,64]{3,2,1,0:T(8,128)(2,1)S(1)}, u32[]{:S(2)}, u32[]{:S(2)}) collective-permute-start(bf16[1,8,128,64]{3,2,1,0:T(8,128)(2,1)S(1)} %fusion.100), channel_id=1, source_target_pairs={{0,8},{8,16},{16,24},{24,32},{32,40},{40,48},{48,56},{56,64},{64,7... | collective-permute-start | bytes 393224 | tf_op jit(solution)/shard_map/while/body/eval_jaxpr/ppermute | solution.py:15
  863.6 12.5 %collective-permute-start.1 = (bf16[1,8,128,64]{3,2,1,0:T(8,128)(2,1)S(1)}, bf16[1,8,128,64]{3,2,1,0:T(8,128)(2,1)S(1)}, u32[]{:S(2)}, u32[]{:S(2)}) collective-permute-start(bf16[1,8,128,64]{3,2,1,0:T(8,128)(2,1)S(1)} %fusion.100), channel_id=1, source_target_pairs={{0,8},{8,16},{16,24},{24,32},{32,40},{40,48},{48,56},{56,64},{64,7... | collective-permute-start | bytes 393224 | tf_op jit(solution)/shard_map/while/body/eval_jaxpr/ppermute | solution.py:15
  876.3 11.7 %collective-permute-start.1 = (bf16[1,8,128,64]{3,2,1,0:T(8,128)(2,1)S(1)}, bf16[1,8,128,64]{3,2,1,0:T(8,128)(2,1)S(1)}, u32[]{:S(2)}, u32[]{:S(2)}) collective-permute-start(bf16[1,8,128,64]{3,2,1,0:T(8,128)(2,1)S(1)} %fusion.100), channel_id=1, source_target_pairs={{0,8},{8,16},{16,24},{24,32},{32,40},{40,48},{48,56},{56,64},{64,7... | collective-permute-start | bytes 393224 | tf_op jit(solution)/shard_map/while/body/eval_jaxpr/ppermute | solution.py:15
  (63 other events, 559.6 us)
Sparse Core Ops, SparseCore 0:
  128.9 35.4 all-gather.1
where the time goes:
time: 1010 us; the launch traced here: 1000 us
  waiting for transfers between devices  521 us (52%)
  starting transfers between devices  279 us (28%)
  local copies, waits for them, and re-layouts  82 us (8%)
  other arithmetic  70.2 us (7%)
  matrix products  34.1 us (3%)
  between operations  14.6 us (1%)
    ppermute x63, waiting for transfers between devices, from_behind(): return lax.ppermute(value, axis, pairs)  429 us
    ppermute x63, starting transfers between devices, from_behind(): return lax.ppermute(value, axis, pairs)  266 us
    add x32, other arithmetic, advance(): return (pair_now[0][..., None, None] * state_now + pair_now[1], state_now)  37.4 us
    all_gather x1, waiting for transfers between devices, shards(): lax.all_gather(residual_grad, 'expert', axis=0, tiled=True)  27.1 us
    all_to_all x1, waiting for transfers between devices, shards(): lax.all_to_all(result.reshape(sender_count, item_count, model_width), 'ex...  26.2 us
    all_to_all x1, waiting for transfers between devices, shards(): lax.all_to_all(send_inputs, 'expert', split_axis=0, concat_axis=0, tiled=...  21.7 us
    mul x32, local copies, waits for them, and re-layouts, advance(): return (pair_now[0][..., None, None] * state_now + pair_now[1], state_now)  20.7 us
  transfers between devices with their start and end apart: 67, of which 66 were waited for; matrix products, arithmetic and copies ran while one was open for 7% of the time, Pallas kernels for 0%

commit v1 on v0

v1 whole, which is shorter than its diff:
```python
import functools

import jax
import jax.numpy as jnp
from jax import lax
from jax.experimental import pallas as pl
from jax.experimental.pallas import tpu as pltpu
from jax.sharding import PartitionSpec as P

P_SIZE = 64
N = 128
KW = 4
SPAN = 128
LANES = 128
MESH = pl.DeviceIdType.MESH
F32 = jnp.float32
BF16 = jnp.bfloat16


def dot(a, b, left, right):
    return lax.dot_general(a, b, (((left,), (right,)), ((), ())), preferred_element_type=F32)


def expert_kernel(
    input_ref,
    grad_ref,
    route_ref,
    up_ref,
    down_ref,
    out_weight_ref,
    residual_ref,
    out_grad_ref,
    inputs,
    grads,
    partial,
    gathered,
    sibling_part,
    far_part,
    near_part,
    summed,
    routes,
    hidden,
    up,
    down,
    out_weight,
    local_sem,
    send_sem,
    recv_sem,
):
    me = lax.axis_index("expert")
    count = lax.axis_size("expert")
    chips = count // 2
    chip, core = me // 2, me % 2
    rows = input_ref.shape[0]
    half = rows // 2
    low, high, whole = pl.ds(0, half), pl.ds(half, half), pl.ds(0, rows)
    other, other_low, other_high = pl.ds(rows, rows), pl.ds(rows, half), pl.ds(rows + half, half)

    def device(chip_step, core_step):
        return ((chip + chip_step) % chips) * 2 + (core + core_step) % 2

    sibling, right, left = device(0, 1), device(1, 0), device(chips - 1, 0)
    copies = {}

    def send(name, source, target_ref, target):
        place = len(copies)
        copies[name] = pltpu.make_async_remote_copy(
            src_ref=source,
            dst_ref=target_ref,
            send_sem=send_sem.at[place],
            recv_sem=recv_sem.at[place],
            device_id={"expert": target},
            device_id_type=MESH,
        )
        copies[name].start()

    def arrived(*names):
        for name in names:
            copies[name].wait_recv()

    loads = []
    for place, (source, target) in enumerate(
        (
            (input_ref, inputs.at[0, whole]),
            (up_ref, up),
            (route_ref.at[me], routes.at[0]),
            (grad_ref, grads.at[0, whole]),
            (down_ref, down),
            (out_weight_ref, out_weight),
        )
    ):
        loads.append(pltpu.make_async_copy(source, target, local_sem.at[place]))
        loads[-1].start()

    barrier = pltpu.get_barrier_semaphore()
    for step in range(1, count):
        pl.semaphore_signal(
            barrier, inc=1, device_id={"expert": (me + step) % count}, device_id_type=MESH
        )
    pl.semaphore_wait(barrier, count - 1)

    def first(tag, source, buffer):
        send(tag + "r1", source.at[low], buffer.at[1, low], right)
        send(tag + "l1", source.at[high], buffer.at[2, high], left)
        send(tag + "s0", source, buffer.at[0, other], sibling)

    def second(tag, source, buffer):
        send(tag + "r2", source.at[high], buffer.at[1, high], right)
        send(tag + "l2", source.at[low], buffer.at[2, low], left)

    def forward(tag, buffer):
        arrived(tag + "r1")
        send(tag + "r3", buffer.at[1, low], buffer.at[3, low], right)
        send(tag + "s1", buffer.at[1, low], buffer.at[1, other_low], sibling)
        arrived(tag + "l1")
        send(tag + "l3", buffer.at[2, high], buffer.at[3, high], left)
        send(tag + "s2", buffer.at[2, high], buffer.at[2, other_high], sibling)

    def share_near(tag, buffer):
        arrived(tag + "r2")
        send(tag + "s3", buffer.at[1, high], buffer.at[1, other_high], sibling)
        arrived(tag + "l2")
        send(tag + "s4", buffer.at[2, low], buffer.at[2, other_low], sibling)

    def share_far(tag, buffer):
        arrived(tag + "r3")
        send(tag + "s5", buffer.at[3, low], buffer.at[3, other_low], sibling)
        arrived(tag + "l3")
        send(tag + "s6", buffer.at[3, high], buffer.at[3, other_high], sibling)

    first("x", input_ref, inputs)
    first("g", grad_ref, grads)
    for chip_step, slot in ((0, 0), (1, 1), (chips - 1, 2), (2, 3)):
        for core_step in range(2):
            if (chip_step, core_step) != (0, 0):
                target = device(chip_step, core_step)
                send(
                    "w%d%d" % (slot, core_step),
                    route_ref.at[target],
                    routes.at[2 * slot + core_step],
                    target,
                )
    second("x", input_ref, inputs)

    def before(slot):
        hidden[slot] = 2.0 * jnp.maximum(dot(inputs[slot], up[...], 1, 0), 0.0)

    def after(slot):
        column = jnp.concatenate(
            [routes[2 * slot].T[:, 0:1], routes[2 * slot + 1].T[:, 0:1]], axis=0
        )
        back = dot(grads[slot], down[...], 1, 1) * column
        inner = (hidden[slot] * back).astype(BF16)
        partial[slot] = dot(inner, up[...], 1, 1).astype(BF16)
        send("p%d" % slot, partial.at[slot, other], sibling_part.at[slot], sibling)

    loads[0].wait()
    loads[1].wait()
    arrived("xs0")
    before(0)
    forward("x", inputs)
    loads[2].wait()
    for slot, core_step in ((0, 1), (1, 0), (1, 1), (2, 0), (2, 1), (3, 0), (3, 1)):
        arrived("w%d%d" % (slot, core_step))
    loads[3].wait()
    loads[4].wait()
    forward("g", grads)
    second("g", grad_ref, grads)
    arrived("gs0")
    after(0)
    share_near("x", inputs)
    arrived("xs1", "xs3")
    before(1)
    arrived("xs2", "xs4")
    before(2)
    share_far("x", inputs)
    arrived("xs5", "xs6")
    before(3)
    share_far("g", grads)
    arrived("gs5", "gs6")
    after(3)
    share_near("g", grads)
    arrived("p3")
    summed[0] = partial[3, whole] + sibling_part[3]
    send("fr", summed.at[0, low], far_part.at[0], right)
    send("fl", summed.at[0, high], far_part.at[1], left)
    arrived("gs2", "gs4")
    after(2)
    arrived("gs1", "gs3")
    after(1)
    arrived("p2")
    summed[1, high] = partial[2, high] + sibling_part[2, high]
    send("nr1", summed.at[1, high], near_part.at[0, high], right)
    arrived("p1")
    summed[2, low] = partial[1, low] + sibling_part[1, low]
    send("nl1", summed.at[2, low], near_part.at[1, low], left)

    def three(a, b, c):
        return (a.astype(F32) + b.astype(F32) + c.astype(F32)).astype(BF16)

    arrived("fr")
    summed[1, low] = three(partial[2, low], sibling_part[2, low], far_part[0])
    send("nr2", summed.at[1, low], near_part.at[0, low], right)
    arrived("fl")
    summed[2, high] = three(partial[1, high], sibling_part[1, high], far_part[1])
    send("nl2", summed.at[2, high], near_part.at[1, high], left)
    loads[5].wait()
    arrived("p0")

    def finish(part):
        gathered[0, part] = (
            grads[0, part].astype(F32)
            + partial[0, part].astype(F32)
            + sibling_part[0, part].astype(F32)
            + near_part[0, part].astype(F32)
            + near_part[1, part].astype(F32)
        ).astype(BF16)

    arrived("nr1", "nl1", "nr2", "nl2")
    finish(low)
    finish(high)
    own = gathered.at[0, whole]
    first("o", own, gathered)
    second("o", own, gathered)
    store = pltpu.make_async_copy(own, residual_ref, local_sem.at[0])
    store.start()

    def project(slot, chip_step):
        product = dot(gathered[slot], out_weight[...], 1, 1).astype(BF16)
        for core_step in range(2):
            start = pl.multiple_of(device(chip_step, core_step) * rows, rows)
            out_grad_ref[pl.ds(start, rows)] = product[core_step * rows : (core_step + 1) * rows]

    forward("o", gathered)
    arrived("os0")
    project(0, 0)
    share_near("o", gathered)
    arrived("os1", "os3")
    project(1, chips - 1)
    arrived("os2", "os4")
    project(2, 1)
    share_far("o", gathered)
    arrived("os5", "os6")
    project(3, 2)
    store.wait()
    for copy in copies.values():
        copy.wait_send()


def expert_part(grad_out, expert_input, expert_index, route_weight, up, down, out_weight):
    count = lax.axis_size("expert")
    rows, width = grad_out.shape
    inner = up.shape[1]
    columns = out_weight.shape[0]
    match = expert_index[None] == jnp.arange(count, dtype=jnp.int32)[:, None, None]
    table = jnp.sum(jnp.where(match, route_weight[None], 0.0), axis=2)
    routes = jnp.broadcast_to(table[:, None, :], (count, 8, rows))
    copies = 64
    hbm = pl.BlockSpec(memory_space=pl.ANY)
    return pl.pallas_call(
        expert_kernel,
        out_shape=(
            jax.ShapeDtypeStruct((rows, width), BF16),
            jax.ShapeDtypeStruct((count * rows, columns), BF16),
        ),
        in_specs=[hbm] * 6,
        out_specs=(hbm, pl.BlockSpec(memory_space=pltpu.VMEM)),
        scratch_shapes=[
            pltpu.VMEM((4, 2 * rows, width), BF16),
            pltpu.VMEM((4, 2 * rows, width), BF16),
            pltpu.VMEM((4, 2 * rows, width), BF16),
            pltpu.VMEM((4, 2 * rows, width), BF16),
            pltpu.VMEM((4, rows, width), BF16),
            pltpu.VMEM((2, rows // 2, width), BF16),
            pltpu.VMEM((2, rows, width), BF16),
            pltpu.VMEM((3, rows, width), BF16),
            pltpu.VMEM((8, 8, rows), F32),
            pltpu.VMEM((4, 2 * rows, inner), F32),
            pltpu.VMEM((width, inner), BF16),
            pltpu.VMEM((inner, width), BF16),
            pltpu.VMEM((columns, width), BF16),
            pltpu.SemaphoreType.DMA((6,)),
            pltpu.SemaphoreType.DMA((copies,)),
            pltpu.SemaphoreType.DMA((copies,)),
        ],
        compiler_params=pltpu.CompilerParams(
            collective_id=1, has_side_effects=True, vmem_limit_bytes=60 * 1024 * 1024
        ),
        name="expert_part",
    )(expert_input, grad_out, routes, up, down, out_weight)


def widen(columns):
    lane = lax.broadcasted_iota(jnp.int32, (columns.shape[0], LANES), 1)
    parts = []
    for pair in range(columns.shape[1] // 2):
        one, two = columns[:, 2 * pair : 2 * pair + 1], columns[:, 2 * pair + 1 : 2 * pair + 2]
        parts.append(jnp.where(lane < P_SIZE, one, two))
    return jnp.concatenate(parts, axis=1)


def head_row(column, width):
    heads = column.shape[0]
    lane = lax.broadcasted_iota(jnp.int32, (heads, width), 1)
    head = lax.broadcasted_iota(jnp.int32, (heads, width), 0)
    chosen = jnp.where(lane // P_SIZE == head, column, 0.0)
    return jnp.broadcast_to(jnp.sum(chosen, axis=0, keepdims=True), (8, width))


def mixer_kernel(
    value_ref,
    taps_ref,
    step_ref,
    decay_ref,
    skip_ref,
    in_basis_ref,
    out_basis_ref,
    out_grad_ref,
    conv_ref,
    in_out_ref,
    out_out_ref,
    mixed,
    weighted,
    grad_weighted,
    slope,
    base,
    in_part,
    out_part,
    value_grad,
    entering,
    leaving,
    running,
    edge,
    sum_rows,
    sum_columns,
    step_columns,
    scale_columns,
    grow_columns,
    block_row,
    prefix_row,
    suffix_row,
    tiles,
    landed,
    outs,
    returned,
    decay_tiles,
    decay_landed,
    halo,
    send_sem,
    recv_sem,
):
    me = lax.axis_index("seq")
    devices = lax.axis_size("seq")
    heads = step_ref.shape[0]
    blocks = step_ref.shape[1] // SPAN
    width = heads * P_SIZE
    length = blocks * SPAN
    strips = width // LANES
    depth = tiles.shape[2]

    barrier = pltpu.get_barrier_semaphore()

    def greet(step, carry):
        pl.semaphore_signal(
            barrier, inc=1, device_id={"seq": (me + step) % devices}, device_id_type=MESH
        )
        return carry

    lax.fori_loop(1, devices, greet, 0)

    lane = lax.broadcasted_iota(jnp.int32, (heads, SPAN), 1)
    ends = []
    for block in range(blocks):
        part = slice(block * SPAN, (block + 1) * SPAN)
        total = decay_ref[:, part]
        shift = 1
        while shift < SPAN:
            total = total + jnp.where(lane >= shift, pltpu.roll(total, shift, 1), 0.0)
            shift *= 2
        last = total[:, SPAN - 1 : SPAN]
        steps = step_ref[:, part]
        sum_rows[block] = total
        sum_columns[block] = total.T
        step_columns[block] = steps.T
        scale_columns[block] = (jnp.exp(last - total) * steps).T
        grow_columns[block] = jnp.exp(total).T
        block_row[block] = head_row(jnp.exp(last), width)
        ends.append(last)
    before = jnp.zeros((heads, 1), F32)
    after = jnp.zeros((heads, 1), F32)
    for block in range(blocks):
        prefix_row[block] = head_row(jnp.exp(before), width)
        before = before + ends[block]
        back = blocks - 1 - block
        suffix_row[back] = head_row(jnp.exp(after), width)
        after = after + ends[back]
    device_row = head_row(jnp.exp(before), width)
    for strip in range(strips):
        decay_tiles[strip] = device_row[:, strip * LANES : (strip + 1) * LANES]

    def rows_of(block):
        return pl.ds(pl.multiple_of(block * SPAN, SPAN), SPAN)

    def remote(place, source, target_ref, target):
        return pltpu.make_async_remote_copy(
            src_ref=source,
            dst_ref=target_ref,
            send_sem=send_sem.at[place],
            recv_sem=recv_sem.at[place],
            device_id={"seq": target},
            device_id_type=MESH,
        )

    def wait_all(place, sent, got):
        remote(place, sent, sent, (me + 1) % devices).wait_send()
        remote(place, got, got, (me + 1) % devices).wait_recv()

    rest = pl.ds(1, devices - 1)

    def scatter_state(way):
        for row in range(N // depth):
            for strip in range(strips):
                tiles[way, row * strips + strip] = running[
                    row * depth : (row + 1) * depth, strip * LANES : (strip + 1) * LANES
                ].astype(BF16)

        def one(step, carry):
            target = (me + step) % devices
            remote(way, tiles.at[way, target], landed.at[way, step], target).start()
            return carry

        lax.fori_loop(1, devices, one, 0)
        landed[way, 0] = tiles[way, me]

    def scan_state(way):
        wait_all(way, tiles.at[way, rest], landed.at[way, rest])
        state = jnp.zeros((depth, LANES), F32)

        def one(turn, state):
            place = turn if way == 0 else devices - 1 - turn
            slot = (me - place + devices) % devices
            outs[way, place] = state.astype(BF16)
            return decay_landed[slot][0:1] * state + landed[way, slot].astype(F32)

        lax.fori_loop(0, devices, one, state)

        def back(step, carry):
            target = (me + step) % devices
            remote(3 + way, outs.at[way, target], returned.at[way, me], target).start()
            return carry

        lax.fori_loop(1, devices, back, 0)
        returned[way, me] = outs[way, me]

    def collect_state(way):
        wait_all(3 + way, outs.at[way, rest], returned.at[way, rest])
        for row in range(N // depth):
            for strip in range(strips):
                edge[
                    way, row * depth : (row + 1) * depth, strip * LANES : (strip + 1) * LANES
                ] = returned[way, row * strips + strip].astype(F32)

    running[...] = jnp.zeros_like(running)

    def ahead(block, carry):
        rows = rows_of(block)
        value = value_ref[rows].astype(F32)
        sigmoid = jax.nn.sigmoid(value)
        act = (value * sigmoid).astype(BF16)
        mixed[rows] = act
        slope[rows] = sigmoid + value * sigmoid * (1.0 - sigmoid)
        scaled = (act.astype(F32) * widen(scale_columns[block])).astype(BF16)
        weighted[rows] = scaled
        entering[block] = running[...]
        running[...] = block_row[block][0:1] * running[...] + dot(in_basis_ref[rows], scaled, 0, 0)
        return carry

    lax.fori_loop(0, blocks, ahead, 0)

    pl.semaphore_wait(barrier, devices - 1)

    def send_decay(step, carry):
        target = (me + step) % devices
        remote(2, decay_tiles.at[target % strips], decay_landed.at[step], target).start()
        return carry

    lax.fori_loop(1, devices, send_decay, 0)
    decay_landed[0] = decay_tiles[me % strips]
    scatter_state(0)

    running[...] = jnp.zeros_like(running)

    def behind(turn, carry):
        block = blocks - 1 - turn
        rows = rows_of(block)
        scaled = (out_grad_ref[rows].astype(F32) * widen(grow_columns[block])).astype(BF16)
        grad_weighted[rows] = scaled
        leaving[block] = running[...]
        running[...] = block_row[block][0:1] * running[...] + dot(
            out_basis_ref[rows], scaled, 0, 0
        )
        return carry

    lax.fori_loop(0, blocks, behind, 0)
    scatter_state(1)
    wait_all(2, decay_landed.at[rest], decay_landed.at[rest])
    scan_state(0)

    lane_row = lax.broadcasted_iota(jnp.int32, (1, LANES), 1)
    left_half = jnp.where(lane_row < P_SIZE, 1.0, 0.0).astype(BF16)
    right_half = jnp.where(lane_row < P_SIZE, 0.0, 1.0).astype(BF16)

    def inside(block, carry):
        rows = rows_of(block)
        in_basis, out_basis = in_basis_ref[rows], out_basis_ref[rows]
        source = lax.broadcasted_iota(jnp.int32, (SPAN, SPAN), 0)
        reader = lax.broadcasted_iota(jnp.int32, (SPAN, SPAN), 1)
        lower = reader >= source
        scores = dot(in_basis, out_basis, 1, 1)
        total = jnp.zeros((SPAN, SPAN), F32)
        for strip in range(strips):
            span = slice(strip * LANES, (strip + 1) * LANES)
            grad_pair = out_grad_ref[rows, span]
            act_pair = mixed[rows, span]
            act_two = jnp.concatenate([act_pair * left_half, act_pair * right_half], axis=0)
            grad_two = jnp.concatenate([grad_pair * left_half, grad_pair * right_half], axis=0)
            grad_mixed = dot(act_two, grad_pair, 1, 1)
            weights = []
            for side in range(2):
                head = 2 * strip + side
                gap = sum_rows[block, head : head + 1, :] - sum_columns[block][:, head : head + 1]
                mask = (
                    jnp.exp(jnp.where(lower, gap, -1e30)) * step_columns[block][:, head : head + 1]
                )
                weights.append((mask * scores).astype(BF16))
                total = total + mask * grad_mixed[side * SPAN : (side + 1) * SPAN]
            inner = dot(jnp.concatenate(weights, axis=1), grad_two, 1, 0)
            base[rows, span] = inner + skip_ref[:, span] * grad_pair.astype(F32)
        in_part[rows] = dot(total.astype(BF16), out_basis, 1, 0)
        out_part[rows] = dot(total.T.astype(BF16), in_basis, 1, 0)
        return carry

    split = blocks // 2
    lax.fori_loop(0, split, inside, 0)
    scan_state(1)
    lax.fori_loop(split, blocks, inside, 0)
    collect_state(0)
    collect_state(1)

    def close(block, carry):
        rows = rows_of(block)
        enter = (entering[block] + prefix_row[block][0:1] * edge[0]).astype(BF16)
        leave = (leaving[block] + suffix_row[block][0:1] * edge[1]).astype(BF16)
        carried = dot(in_basis_ref[rows], leave, 1, 0)
        value_grad[rows] = (base[rows] + widen(scale_columns[block]) * carried) * slope[rows]
        in_out_ref[rows] = (in_part[rows] + dot(weighted[rows], leave, 1, 1)).astype(BF16)
        out_out_ref[rows] = (out_part[rows] + dot(grad_weighted[rows], enter, 1, 1)).astype(BF16)
        return carry

    close(0, 0)
    ahead_rows = remote(5, value_grad.at[pl.ds(0, 8)], halo, (me + devices - 1) % devices)
    ahead_rows.start()
    lax.fori_loop(1, blocks, close, 0)
    ahead_rows.wait()
    value_grad[pl.ds(length, 8)] = jnp.where(me == devices - 1, 0.0, halo[...])

    def filtered(block, carry):
        start = pl.multiple_of(block * SPAN, SPAN)
        window = value_grad[pl.ds(start, SPAN + 8)]
        summed = taps_ref[0:1] * window[0:SPAN]
        for tap in range(1, KW):
            summed = summed + taps_ref[tap : tap + 1] * window[tap : tap + SPAN]
        conv_ref[pl.ds(start, SPAN)] = summed.astype(BF16)
        return carry

    lax.fori_loop(0, blocks, filtered, 0)


def mixer_part(value, taps, step, decay, skip, in_basis, out_basis, out_grad):
    devices = lax.axis_size("seq")
    heads, length = step.shape
    blocks = length // SPAN
    width = heads * P_SIZE
    strips = width // LANES
    depth = N * strips // devices
    skip_row = jnp.repeat(skip, P_SIZE)[None]
    vmem = pl.BlockSpec(memory_space=pltpu.VMEM)
    return pl.pallas_call(
        mixer_kernel,
        out_shape=(
            jax.ShapeDtypeStruct((length, width), BF16),
            jax.ShapeDtypeStruct((length, N), BF16),
            jax.ShapeDtypeStruct((length, N), BF16),
        ),
        in_specs=[vmem] * 8,
        out_specs=(vmem,) * 3,
        scratch_shapes=[
            pltpu.VMEM((length, width), BF16),
            pltpu.VMEM((length, width), BF16),
            pltpu.VMEM((length, width), BF16),
            pltpu.VMEM((length, width), F32),
            pltpu.VMEM((length, width), F32),
            pltpu.VMEM((length, N), F32),
            pltpu.VMEM((length, N), F32),
            pltpu.VMEM((length + 8, width), F32),
            pltpu.VMEM((blocks, N, width), F32),
            pltpu.VMEM((blocks, N, width), F32),
            pltpu.VMEM((N, width), F32),
            pltpu.VMEM((2, N, width), F32),
            pltpu.VMEM((blocks, heads, SPAN), F32),
            pltpu.VMEM((blocks, SPAN, heads), F32),
            pltpu.VMEM((blocks, SPAN, heads), F32),
            pltpu.VMEM((blocks, SPAN, heads), F32),
            pltpu.VMEM((blocks, SPAN, heads), F32),
            pltpu.VMEM((blocks, 8, width), F32),
            pltpu.VMEM((blocks, 8, width), F32),
            pltpu.VMEM((blocks, 8, width), F32),
            pltpu.VMEM((2, devices, depth, LANES), BF16),
            pltpu.VMEM((2, devices, depth, LANES), BF16),
            pltpu.VMEM((2, devices, depth, LANES), BF16),
            pltpu.VMEM((2, devices, depth, LANES), BF16),
            pltpu.VMEM((strips, 8, LANES), F32),
            pltpu.VMEM((devices, 8, LANES), F32),
            pltpu.VMEM((8, width), F32),
            pltpu.SemaphoreType.DMA((6,)),
            pltpu.SemaphoreType.DMA((6,)),
        ],
        compiler_params=pltpu.CompilerParams(
            collective_id=2, has_side_effects=True, vmem_limit_bytes=60 * 1024 * 1024
        ),
        name="mixer_part",
    )(value, taps, step, decay, skip_row, in_basis, out_basis, out_grad)


def shards(
    grad_out,
    expert_input,
    expert_index,
    route_weight,
    up_weight,
    down_weight,
    out_weight,
    conv_value,
    conv_weight,
    step_size,
    log_decay,
    skip_gain,
    input_basis,
    output_basis,
):
    residual_grad, out_grad = expert_part(
        grad_out,
        expert_input,
        expert_index,
        route_weight,
        up_weight[0],
        down_weight[0],
        out_weight,
    )
    conv_grad, in_grad, out_part = mixer_part(
        conv_value,
        conv_weight,
        step_size,
        log_decay,
        skip_gain,
        input_basis,
        output_basis,
        out_grad,
    )
    return (residual_grad, conv_grad, in_grad, out_part)


def solution(mesh):
    in_specs = (
        P(("seq", "expert"), None),
        P(("seq", "expert"), None),
        P(("seq", "expert"), None),
        P(("seq", "expert"), None),
        P("expert", None, None),
        P("expert", None, None),
        P("expert", None),
        P("seq", "expert"),
        P(None, "expert"),
        P("expert", "seq"),
        P("expert", "seq"),
        P("expert"),
        P("seq", "expert"),
        P("seq", "expert"),
    )
    out_specs = (
        P(("seq", "expert"), None),
        P("seq", "expert"),
        P("seq", "expert"),
        P("seq", "expert"),
    )
    return jax.shard_map(shards, mesh=mesh, in_specs=in_specs, out_specs=out_specs, check_vma=False)
```

time: 1010 us -> 130 us (0.13)
  waiting for transfers between devices: 521 us -> 0 us
  starting transfers between devices: 279 us -> 0 us
  Pallas kernels: 0 us -> 119 us
  local copies, waits for them, and re-layouts: 82 us -> 7.61 us
  other arithmetic: 70.2 us -> 0.7 us
  matrix products: 34.1 us -> 0 us
  between operations: 14.6 us -> 0.67 us
    ppermute x63 -> x0, waiting for transfers between devices: 429 us -> none  [from_behind(): return lax.ppermute(value, axis, pairs)]
    ppermute x63 -> x0, starting transfers between devices: 266 us -> none  [from_behind(): return lax.ppermute(value, axis, pairs)]
    pallas_call x0 -> x2, Pallas kernels: none -> 119 us  [the longest x1 83.2 us: expert_part(): pl.pallas_call(expert_kernel, out_shape=(jax.ShapeDtypeStruct((rows, widt...]
    all_to_all x3 -> x0, waiting for transfers between devices: 65.4 us -> none  [the longest x1 26.2 us: shards(): lax.all_to_all(result.reshape(sender_count, item_count, model_width), 'ex...]
    add x32 -> x0, other arithmetic: 37.4 us -> none  [advance(): return (pair_now[0][..., None, None] * state_now + pair_now[1], state_now)]
    dot_general x13 -> x0, matrix products: 34.1 us -> none  [the longest x1 7.33 us: expert_rows(): jnp.dot(inner_grad, up_matrix.T, preferred_element_type=jnp.float32)]
    all_gather x1 -> x0, waiting for transfers between devices: 27.1 us -> none  [shards(): lax.all_gather(residual_grad, 'expert', axis=0, tiled=True)]
    mul x36 -> x0, local copies, waits for them, and re-layouts: 21.6 us -> none  [the longest x32 20.7 us: advance(): return (pair_now[0][..., None, None] * state_now + pair_now[1], state_now)]
  transfers between devices with their start and end apart: 67 -> 0, of which waited for: 66 -> 0; matrix products, arithmetic and copies ran while one was open for 7% -> 0% of each run, Pallas kernels for 0% -> 0%
where the time goes in v1:
time: 130 us; the launch traced here: 128 us
  Pallas kernels  119 us (92%)
  local copies, waits for them, and re-layouts  7.61 us (6%)
    pallas_call x1, Pallas kernels, expert_part(): pl.pallas_call(expert_kernel, out_shape=(jax.ShapeDtypeStruct((rows, widt...  83.2 us
    pallas_call x1, Pallas kernels, mixer_part(): pl.pallas_call(mixer_kernel, out_shape=(jax.ShapeDtypeStruct((length, wid...  36.3 us
    unnamed x8, local copies, waits for them, and re-layouts  5.61 us

profile of v1, /device:TPU:24, one launch (start us, length us, event | category | flops | bytes accessed | tf_op | source)
XLA Modules:
  0.0 128.4 jit_solution(5626671225545781551)
XLA Ops:
  0.6 0.7 select_reduce_fusion
  1.3 0.7 broadcast_in_dim.27
  2.1 0.7 broadcast_in_dim_reshape.3.skip_ref
  2.7 0.6 broadcast_in_dim.26.route_ref
  3.3 83.2 %expert_part.1 = (bf16[128,2048]{1,0:T(8,128)(2,1)}, bf16[1024,512]{1,0:T(8,128)(2,1)}) custom-call(bf16[128,2048]{1,0:T(8,128)(2,1)} %input_ref.1, bf16[128,2048]{1,0:T(8,128)(2,1)} %grad_ref.1, f32[8,8,128]{2,1,0:T(8,128)} %broadcast_in_dim.26.route_ref, bf16[2048,768]{1,0:T(8,128)(2,1)} %bitcast.2, bf16[768,2048]{1,0:T(8,128)(2,1)} %bitcast.3, ...), custom_call_target="tpu_custom_call" | custom-call | tf_op jit(solution)/shard_map/expert_part/pallas_call | solution.py:260
  86.5 36.3 %mixer_part.1 = (bf16[1024,512]{1,0:T(8,128)(2,1)}, bf16[1024,128]{1,0:T(8,128)(2,1)}, bf16[1024,128]{1,0:T(8,128)(2,1)}) custom-call(bf16[1024,512]{1,0:T(8,128)(2,1)} %value_ref.1, f32[4,512]{1,0:T(4,128)} %taps_ref.1, f32[8,1024]{1,0:T(8,128)} %step_ref.1, f32[8,1024]{1,0:T(8,128)} %decay_ref.1, f32[1,512]{1,0:T(1,128)} %broadcast_in_dim_reshape.3.skip_ref, ...), custom_call_target="tpu_custom_call" | custom-call | tf_op jit(solution)/shard_map/mixer_part/pallas_call | solution.py:588
  122.8 0.0 copy-start.1
  122.8 0.0 copy-start
  122.8 1.9 %copy.24 = bf16[128,2048]{1,0:T(8,128)(2,1)} copy(bf16[128,2048]{1,0:T(8,128)(2,1)} %get-tuple-element.18) | data formatting | bytes 1048576
  124.8 2.3 %copy.25 = bf16[1024,512]{1,0:T(8,128)(2,1)} copy(bf16[1024,512]{1,0:T(8,128)(2,1)} %get-tuple-element.19) | data formatting | bytes 2097152
  127.0 0.0 copy-done.1
  127.0 0.7 copy.26
  127.7 0.0 copy-done
  127.7 0.7 copy.27
Async XLA Ops:
  122.8 4.2 %copy-start.1 = (bf16[1024,128]{1,0:T(8,128)(2,1)S(1)}, bf16[1024,128]{1,0:T(8,128)(2,1)}, u32[]{:S(2)}) copy-start(bf16[1024,128]{1,0:T(8,128)(2,1)} %get-tuple-element.20) | copy-start | bytes 786436
  122.8 4.9 %copy-start = (bf16[1024,128]{1,0:T(8,128)(2,1)S(1)}, bf16[1024,128]{1,0:T(8,128)(2,1)}, u32[]{:S(2)}) copy-start(bf16[1024,128]{1,0:T(8,128)(2,1)} %get-tuple-element.21) | copy-start | bytes 786436

commit v2 on v1

v2 whole, which is shorter than its diff:
```python
import functools

import jax
import jax.numpy as jnp
from jax import lax
from jax.experimental import pallas as pl
from jax.experimental.pallas import tpu as pltpu
from jax.sharding import PartitionSpec as P

P_SIZE = 64
N = 128
KW = 4
SPAN = 128
LANES = 128
MESH = pl.DeviceIdType.MESH
F32 = jnp.float32
BF16 = jnp.bfloat16


def dot(a, b, left, right):
    return lax.dot_general(a, b, (((left,), (right,)), ((), ())), preferred_element_type=F32)


def widen(columns):
    lane = lax.broadcasted_iota(jnp.int32, (columns.shape[0], LANES), 1)
    parts = []
    for pair in range(columns.shape[1] // 2):
        one, two = columns[:, 2 * pair : 2 * pair + 1], columns[:, 2 * pair + 1 : 2 * pair + 2]
        parts.append(jnp.where(lane < P_SIZE, one, two))
    return jnp.concatenate(parts, axis=1)


def head_row(column, width):
    heads = column.shape[0]
    lane = lax.broadcasted_iota(jnp.int32, (heads, width), 1)
    head = lax.broadcasted_iota(jnp.int32, (heads, width), 0)
    chosen = jnp.where(lane // P_SIZE == head, column, 0.0)
    return jnp.broadcast_to(jnp.sum(chosen, axis=0, keepdims=True), (8, width))


def layer_kernel(
    input_ref,
    grad_ref,
    route_ref,
    up_ref,
    down_ref,
    out_weight_ref,
    value_hbm,
    in_basis_hbm,
    out_basis_hbm,
    taps_ref,
    step_ref,
    decay_ref,
    skip_ref,
    residual_ref,
    conv_ref,
    in_out_ref,
    out_out_ref,
    inputs,
    grads,
    partial,
    gathered,
    sibling_part,
    far_part,
    near_part,
    summed,
    routes,
    hidden,
    up,
    down,
    out_weight,
    out_grad,
    value_ref,
    in_basis_ref,
    out_basis_ref,
    mixed,
    weighted,
    grad_weighted,
    slope,
    masks,
    weights,
    in_part,
    out_part,
    value_grad,
    entering,
    leaving,
    running,
    edge,
    sum_rows,
    sum_columns,
    step_columns,
    scale_columns,
    grow_columns,
    block_row,
    prefix_row,
    suffix_row,
    tiles,
    landed,
    outs,
    returned,
    decay_tiles,
    decay_landed,
    halo,
    local_sem,
    send_sem,
    recv_sem,
    seq_send,
    seq_recv,
):
    here = lax.axis_index("seq")
    devices = lax.axis_size("seq")
    heads = step_ref.shape[0]
    blocks = step_ref.shape[1] // SPAN
    width = heads * P_SIZE
    length = blocks * SPAN
    strips = width // LANES
    depth = tiles.shape[2]

    me = lax.axis_index("expert")
    count = lax.axis_size("expert")
    chips = count // 2
    chip, core = me // 2, me % 2
    rows = input_ref.shape[0]
    half = rows // 2
    low, high, whole = pl.ds(0, half), pl.ds(half, half), pl.ds(0, rows)
    other, other_low, other_high = pl.ds(rows, rows), pl.ds(rows, half), pl.ds(rows + half, half)

    def device(chip_step, core_step):
        return ((chip + chip_step) % chips) * 2 + (core + core_step) % 2

    sibling, right, left = device(0, 1), device(1, 0), device(chips - 1, 0)
    copies = {}

    def send(name, source, target_ref, target):
        place = len(copies)
        copies[name] = pltpu.make_async_remote_copy(
            src_ref=source,
            dst_ref=target_ref,
            send_sem=send_sem.at[place],
            recv_sem=recv_sem.at[place],
            device_id={"expert": target},
            device_id_type=MESH,
        )
        copies[name].start()

    def arrived(*names):
        for name in names:
            copies[name].wait_recv()

    loads = []
    for place, (source, target) in enumerate(
        (
            (input_ref, inputs.at[0, whole]),
            (up_ref, up),
            (route_ref.at[me], routes.at[0]),
            (grad_ref, grads.at[0, whole]),
            (down_ref, down),
            (out_weight_ref, out_weight),
            (value_hbm, value_ref),
            (in_basis_hbm, in_basis_ref),
            (out_basis_hbm, out_basis_ref),
        )
    ):
        loads.append(pltpu.make_async_copy(source, target, local_sem.at[place]))
        loads[-1].start()

    barrier = pltpu.get_barrier_semaphore()
    for step in range(1, count):
        pl.semaphore_signal(
            barrier, inc=1, device_id={"expert": (me + step) % count}, device_id_type=MESH
        )

    def greet(step, carry):
        pl.semaphore_signal(
            barrier, inc=1, device_id={"seq": (here + step) % devices}, device_id_type=MESH
        )
        return carry

    lax.fori_loop(1, devices, greet, 0)
    pl.semaphore_wait(barrier, count + devices - 2)

    def first(tag, source, buffer):
        send(tag + "r1", source.at[low], buffer.at[1, low], right)
        send(tag + "l1", source.at[high], buffer.at[2, high], left)
        send(tag + "s0", source, buffer.at[0, other], sibling)

    def second(tag, source, buffer):
        send(tag + "r2", source.at[high], buffer.at[1, high], right)
        send(tag + "l2", source.at[low], buffer.at[2, low], left)

    def forward(tag, buffer):
        arrived(tag + "r1")
        send(tag + "r3", buffer.at[1, low], buffer.at[3, low], right)
        send(tag + "s1", buffer.at[1, low], buffer.at[1, other_low], sibling)
        arrived(tag + "l1")
        send(tag + "l3", buffer.at[2, high], buffer.at[3, high], left)
        send(tag + "s2", buffer.at[2, high], buffer.at[2, other_high], sibling)

    def share_near(tag, buffer):
        arrived(tag + "r2")
        send(tag + "s3", buffer.at[1, high], buffer.at[1, other_high], sibling)
        arrived(tag + "l2")
        send(tag + "s4", buffer.at[2, low], buffer.at[2, other_low], sibling)

    def share_far(tag, buffer):
        arrived(tag + "r3")
        send(tag + "s5", buffer.at[3, low], buffer.at[3, other_low], sibling)
        arrived(tag + "l3")
        send(tag + "s6", buffer.at[3, high], buffer.at[3, other_high], sibling)

    first("x", input_ref, inputs)
    first("g", grad_ref, grads)
    for chip_step, slot in ((0, 0), (1, 1), (chips - 1, 2), (2, 3)):
        for core_step in range(2):
            if (chip_step, core_step) != (0, 0):
                target = device(chip_step, core_step)
                send(
                    "w%d%d" % (slot, core_step),
                    route_ref.at[target],
                    routes.at[2 * slot + core_step],
                    target,
                )
    second("x", input_ref, inputs)

    lane = lax.broadcasted_iota(jnp.int32, (heads, SPAN), 1)
    ends = []
    for block in range(blocks):
        part = slice(block * SPAN, (block + 1) * SPAN)
        total = decay_ref[:, part]
        shift = 1
        while shift < SPAN:
            total = total + jnp.where(lane >= shift, pltpu.roll(total, shift, 1), 0.0)
            shift *= 2
        last = total[:, SPAN - 1 : SPAN]
        steps = step_ref[:, part]
        sum_rows[block] = total
        sum_columns[block] = total.T
        step_columns[block] = steps.T
        scale_columns[block] = (jnp.exp(last - total) * steps).T
        grow_columns[block] = jnp.exp(total).T
        block_row[block] = head_row(jnp.exp(last), width)
        ends.append(last)
    before = jnp.zeros((heads, 1), F32)
    after = jnp.zeros((heads, 1), F32)
    for block in range(blocks):
        prefix_row[block] = head_row(jnp.exp(before), width)
        before = before + ends[block]
        back = blocks - 1 - block
        suffix_row[back] = head_row(jnp.exp(after), width)
        after = after + ends[back]
    device_row = head_row(jnp.exp(before), width)
    for strip in range(strips):
        decay_tiles[strip] = device_row[:, strip * LANES : (strip + 1) * LANES]

    def rows_of(block):
        return pl.ds(pl.multiple_of(block * SPAN, SPAN), SPAN)

    def remote(place, source, target_ref, target):
        return pltpu.make_async_remote_copy(
            src_ref=source,
            dst_ref=target_ref,
            send_sem=seq_send.at[place],
            recv_sem=seq_recv.at[place],
            device_id={"seq": target},
            device_id_type=MESH,
        )

    def wait_all(place, sent, got):
        remote(place, sent, sent, (here + 1) % devices).wait_send()
        remote(place, got, got, (here + 1) % devices).wait_recv()

    rest = pl.ds(1, devices - 1)

    def scatter_state(way):
        for row in range(N // depth):
            for strip in range(strips):
                tiles[way, row * strips + strip] = running[
                    row * depth : (row + 1) * depth, strip * LANES : (strip + 1) * LANES
                ].astype(BF16)

        def one(step, carry):
            target = (here + step) % devices
            remote(way, tiles.at[way, target], landed.at[way, step], target).start()
            return carry

        lax.fori_loop(1, devices, one, 0)
        landed[way, 0] = tiles[way, here]

    def scan_state(way):
        wait_all(way, tiles.at[way, rest], landed.at[way, rest])
        state = jnp.zeros((depth, LANES), F32)

        def one(turn, state):
            place = turn if way == 0 else devices - 1 - turn
            slot = (here - place + devices) % devices
            outs[way, place] = state.astype(BF16)
            return decay_landed[slot][0:1] * state + landed[way, slot].astype(F32)

        lax.fori_loop(0, devices, one, state)

        def back(step, carry):
            target = (here + step) % devices
            remote(3 + way, outs.at[way, target], returned.at[way, here], target).start()
            return carry

        lax.fori_loop(1, devices, back, 0)
        returned[way, here] = outs[way, here]

    def collect_state(way):
        wait_all(3 + way, outs.at[way, rest], returned.at[way, rest])
        for row in range(N // depth):
            for strip in range(strips):
                edge[
                    way, row * depth : (row + 1) * depth, strip * LANES : (strip + 1) * LANES
                ] = returned[way, row * strips + strip].astype(F32)


    lane_row = lax.broadcasted_iota(jnp.int32, (1, LANES), 1)
    left_half = jnp.where(lane_row < P_SIZE, 1.0, 0.0).astype(BF16)
    right_half = jnp.where(lane_row < P_SIZE, 0.0, 1.0).astype(BF16)

    def weigh(block, carry):
        rows = rows_of(block)
        source = lax.broadcasted_iota(jnp.int32, (SPAN, SPAN), 0)
        reader = lax.broadcasted_iota(jnp.int32, (SPAN, SPAN), 1)
        lower = reader >= source
        scores = dot(in_basis_ref[rows], out_basis_ref[rows], 1, 1)
        for head in range(heads):
            gap = sum_rows[block, head : head + 1, :] - sum_columns[block][:, head : head + 1]
            mask = jnp.exp(jnp.where(lower, gap, -1e30)) * step_columns[block][:, head : head + 1]
            masks[block, head] = mask
            weights[block, :, head * SPAN : (head + 1) * SPAN] = (mask * scores).astype(BF16)
        return carry

    def local_start(block):
        rows = rows_of(block)
        scaled = (out_grad[rows].astype(F32) * widen(grow_columns[block])).astype(BF16)
        grad_weighted[rows] = scaled
        leaving[block] = dot(out_basis_ref[rows], scaled, 0, 0)

    def inside(block):
        rows = rows_of(block)
        in_basis, out_basis = in_basis_ref[rows], out_basis_ref[rows]
        total = jnp.zeros((SPAN, SPAN), F32)
        skip_row = widen(skip_ref[...])
        for strip in range(strips):
            span = slice(strip * LANES, (strip + 1) * LANES)
            grad_pair = out_grad[rows, span]
            act_pair = mixed[rows, span]
            act_two = jnp.concatenate([act_pair * left_half, act_pair * right_half], axis=0)
            grad_two = jnp.concatenate([grad_pair * left_half, grad_pair * right_half], axis=0)
            grad_mixed = dot(act_two, grad_pair, 1, 1)
            for side in range(2):
                total = total + masks[block, 2 * strip + side] * (
                    grad_mixed[side * SPAN : (side + 1) * SPAN]
                )
            pair = weights[block, :, 2 * strip * SPAN : 2 * (strip + 1) * SPAN]
            value_grad[rows, span] = dot(pair, grad_two, 1, 0) + skip_row[
                :, span
            ] * grad_pair.astype(F32)
        in_part[rows] = dot(total.astype(BF16), out_basis, 1, 0)
        out_part[rows] = dot(total.T.astype(BF16), in_basis, 1, 0)

    def chain_back():
        running[...] = jnp.zeros_like(running)

        def behind(turn, carry):
            block = blocks - 1 - turn
            added = leaving[block]
            leaving[block] = running[...]
            running[...] = block_row[block][0:1] * running[...] + added
            return carry

        lax.fori_loop(0, blocks, behind, 0)

    def close_out(block, carry):
        rows = rows_of(block)
        enter = (entering[block] + prefix_row[block][0:1] * edge[0]).astype(BF16)
        out_out_ref[rows] = (out_part[rows] + dot(grad_weighted[rows], enter, 1, 1)).astype(BF16)
        return carry

    def close(block, carry):
        rows = rows_of(block)
        leave = (leaving[block] + suffix_row[block][0:1] * edge[1]).astype(BF16)
        carried = dot(in_basis_ref[rows], leave, 1, 0)
        value_grad[rows] = (value_grad[rows] + widen(scale_columns[block]) * carried) * slope[rows]
        in_out_ref[rows] = (in_part[rows] + dot(weighted[rows], leave, 1, 1)).astype(BF16)
        return carry

    def inner_blocks(chip_step, work):
        def one(core_step, carry):
            work(device(chip_step, core_step))
            return carry

        lax.fori_loop(0, 2, one, 0)

    def both(block):
        local_start(block)
        inside(block)

    def before(slot):
        hidden[slot] = 2.0 * jnp.maximum(dot(inputs[slot], up[...], 1, 0), 0.0)

    def after(slot):
        column = jnp.concatenate(
            [routes[2 * slot].T[:, 0:1], routes[2 * slot + 1].T[:, 0:1]], axis=0
        )
        back = dot(grads[slot], down[...], 1, 1) * column
        inner = (hidden[slot] * back).astype(BF16)
        partial[slot] = dot(inner, up[...], 1, 1).astype(BF16)
        send("p%d" % slot, partial.at[slot, other], sibling_part.at[slot], sibling)

    loads[0].wait()
    loads[1].wait()
    arrived("xs0")
    before(0)
    forward("x", inputs)
    for place in (6, 7, 8):
        loads[place].wait()
    running[...] = jnp.zeros_like(running)

    def ahead(block, carry):
        rows = rows_of(block)
        value = value_ref[rows].astype(F32)
        sigmoid = jax.nn.sigmoid(value)
        act = (value * sigmoid).astype(BF16)
        mixed[rows] = act
        slope[rows] = sigmoid + value * sigmoid * (1.0 - sigmoid)
        scaled = (act.astype(F32) * widen(scale_columns[block])).astype(BF16)
        weighted[rows] = scaled
        entering[block] = running[...]
        running[...] = block_row[block][0:1] * running[...] + dot(in_basis_ref[rows], scaled, 0, 0)
        return carry

    lax.fori_loop(0, blocks, ahead, 0)

    def send_decay(step, carry):
        target = (here + step) % devices
        remote(2, decay_tiles.at[target % strips], decay_landed.at[step], target).start()
        return carry

    lax.fori_loop(1, devices, send_decay, 0)
    decay_landed[0] = decay_tiles[here % strips]
    scatter_state(0)

    loads[2].wait()
    for slot, core_step in ((0, 1), (1, 0), (1, 1), (2, 0), (2, 1), (3, 0), (3, 1)):
        arrived("w%d%d" % (slot, core_step))
    loads[3].wait()
    loads[4].wait()
    forward("g", grads)
    second("g", grad_ref, grads)
    arrived("gs0")
    after(0)
    lax.fori_loop(0, blocks, weigh, 0)
    share_near("x", inputs)
    arrived("xs1", "xs3")
    before(1)
    arrived("xs2", "xs4")
    before(2)
    share_far("x", inputs)
    arrived("xs5", "xs6")
    before(3)
    wait_all(2, decay_landed.at[rest], decay_landed.at[rest])
    scan_state(0)
    share_far("g", grads)
    arrived("gs5", "gs6")
    after(3)
    share_near("g", grads)
    arrived("p3")
    summed[0] = partial[3, whole] + sibling_part[3]
    send("fr", summed.at[0, low], far_part.at[0], right)
    send("fl", summed.at[0, high], far_part.at[1], left)
    arrived("gs2", "gs4")
    after(2)
    arrived("gs1", "gs3")
    after(1)
    arrived("p2")
    summed[1, high] = partial[2, high] + sibling_part[2, high]
    send("nr1", summed.at[1, high], near_part.at[0, high], right)
    arrived("p1")
    summed[2, low] = partial[1, low] + sibling_part[1, low]
    send("nl1", summed.at[2, low], near_part.at[1, low], left)

    def three(a, b, c):
        return (a.astype(F32) + b.astype(F32) + c.astype(F32)).astype(BF16)

    arrived("fr")
    summed[1, low] = three(partial[2, low], sibling_part[2, low], far_part[0])
    send("nr2", summed.at[1, low], near_part.at[0, low], right)
    arrived("fl")
    summed[2, high] = three(partial[1, high], sibling_part[1, high], far_part[1])
    send("nl2", summed.at[2, high], near_part.at[1, high], left)
    loads[5].wait()
    arrived("p0")

    def finish(part):
        gathered[0, part] = (
            grads[0, part].astype(F32)
            + partial[0, part].astype(F32)
            + sibling_part[0, part].astype(F32)
            + near_part[0, part].astype(F32)
            + near_part[1, part].astype(F32)
        ).astype(BF16)

    arrived("nr1", "nl1", "nr2", "nl2")
    finish(low)
    finish(high)
    own = gathered.at[0, whole]
    first("o", own, gathered)
    second("o", own, gathered)
    store = pltpu.make_async_copy(own, residual_ref, local_sem.at[0])
    store.start()

    def project(slot, chip_step):
        product = dot(gathered[slot], out_weight[...], 1, 1).astype(BF16)
        for core_step in range(2):
            start = pl.multiple_of(device(chip_step, core_step) * rows, rows)
            out_grad[pl.ds(start, rows)] = product[core_step * rows : (core_step + 1) * rows]

    arrived("os0")
    project(0, 0)
    inner_blocks(0, both)
    forward("o", gathered)
    share_near("o", gathered)
    arrived("os1", "os3")
    project(1, chips - 1)
    inner_blocks(chips - 1, both)
    arrived("os2", "os4")
    project(2, 1)
    inner_blocks(1, both)
    share_far("o", gathered)
    arrived("os5", "os6")
    project(3, 2)
    inner_blocks(2, local_start)
    chain_back()
    scatter_state(1)
    inner_blocks(2, inside)
    scan_state(1)
    collect_state(0)
    lax.fori_loop(0, blocks, close_out, 0)
    collect_state(1)
    close(0, 0)
    ahead_rows = remote(5, value_grad.at[pl.ds(0, 8)], halo, (here + devices - 1) % devices)
    ahead_rows.start()
    lax.fori_loop(1, blocks, close, 0)
    ahead_rows.wait()
    value_grad[pl.ds(length, 8)] = jnp.where(here == devices - 1, 0.0, halo[...])

    def filtered(block, carry):
        start = pl.multiple_of(block * SPAN, SPAN)
        window = value_grad[pl.ds(start, SPAN + 8)]
        summed = taps_ref[0:1] * window[0:SPAN]
        for tap in range(1, KW):
            summed = summed + taps_ref[tap : tap + 1] * window[tap : tap + SPAN]
        conv_ref[pl.ds(start, SPAN)] = summed.astype(BF16)
        return carry

    lax.fori_loop(0, blocks, filtered, 0)


    store.wait()
    for copy in copies.values():
        copy.wait_send()


def layer_part(
    grad_out,
    expert_input,
    expert_index,
    route_weight,
    up,
    down,
    out_weight,
    value,
    taps,
    step,
    decay,
    skip,
    in_basis,
    out_basis,
):
    count = lax.axis_size("expert")
    rows, wide = grad_out.shape
    inner = up.shape[1]
    match = expert_index[None] == jnp.arange(count, dtype=jnp.int32)[:, None, None]
    table = jnp.sum(jnp.where(match, route_weight[None], 0.0), axis=2)
    routes = jnp.broadcast_to(table[:, None, :], (count, 8, rows))
    copies = 64
    devices = lax.axis_size("seq")
    heads, length = step.shape
    blocks = length // SPAN
    width = heads * P_SIZE
    strips = width // LANES
    depth = N * strips // devices
    hbm = pl.BlockSpec(memory_space=pl.ANY)
    vmem = pl.BlockSpec(memory_space=pltpu.VMEM)
    return pl.pallas_call(
        layer_kernel,
        out_shape=(
            jax.ShapeDtypeStruct((rows, wide), BF16),
            jax.ShapeDtypeStruct((length, width), BF16),
            jax.ShapeDtypeStruct((length, N), BF16),
            jax.ShapeDtypeStruct((length, N), BF16),
        ),
        in_specs=[hbm] * 9 + [vmem] * 4,
        out_specs=(hbm, vmem, vmem, vmem),
        scratch_shapes=[
            pltpu.VMEM((4, 2 * rows, wide), BF16),
            pltpu.VMEM((4, 2 * rows, wide), BF16),
            pltpu.VMEM((4, 2 * rows, wide), BF16),
            pltpu.VMEM((4, 2 * rows, wide), BF16),
            pltpu.VMEM((4, rows, wide), BF16),
            pltpu.VMEM((2, rows // 2, wide), BF16),
            pltpu.VMEM((2, rows, wide), BF16),
            pltpu.VMEM((3, rows, wide), BF16),
            pltpu.VMEM((8, 8, rows), F32),
            pltpu.VMEM((4, 2 * rows, inner), F32),
            pltpu.VMEM((wide, inner), BF16),
            pltpu.VMEM((inner, wide), BF16),
            pltpu.VMEM((width, wide), BF16),
            pltpu.VMEM((length, width), BF16),
            pltpu.VMEM((length, width), BF16),
            pltpu.VMEM((length, N), BF16),
            pltpu.VMEM((length, N), BF16),
            pltpu.VMEM((length, width), BF16),
            pltpu.VMEM((length, width), BF16),
            pltpu.VMEM((length, width), BF16),
            pltpu.VMEM((length, width), F32),
            pltpu.VMEM((blocks, heads, SPAN, SPAN), F32),
            pltpu.VMEM((blocks, SPAN, heads * SPAN), BF16),
            pltpu.VMEM((length, N), F32),
            pltpu.VMEM((length, N), F32),
            pltpu.VMEM((length + 8, width), F32),
            pltpu.VMEM((blocks, N, width), F32),
            pltpu.VMEM((blocks, N, width), F32),
            pltpu.VMEM((N, width), F32),
            pltpu.VMEM((2, N, width), F32),
            pltpu.VMEM((blocks, heads, SPAN), F32),
            pltpu.VMEM((blocks, SPAN, heads), F32),
            pltpu.VMEM((blocks, SPAN, heads), F32),
            pltpu.VMEM((blocks, SPAN, heads), F32),
            pltpu.VMEM((blocks, SPAN, heads), F32),
            pltpu.VMEM((blocks, 8, width), F32),
            pltpu.VMEM((blocks, 8, width), F32),
            pltpu.VMEM((blocks, 8, width), F32),
            pltpu.VMEM((2, devices, depth, LANES), BF16),
            pltpu.VMEM((2, devices, depth, LANES), BF16),
            pltpu.VMEM((2, devices, depth, LANES), BF16),
            pltpu.VMEM((2, devices, depth, LANES), BF16),
            pltpu.VMEM((strips, 8, LANES), F32),
            pltpu.VMEM((devices, 8, LANES), F32),
            pltpu.VMEM((8, width), F32),
            pltpu.SemaphoreType.DMA((9,)),
            pltpu.SemaphoreType.DMA((copies,)),
            pltpu.SemaphoreType.DMA((copies,)),
            pltpu.SemaphoreType.DMA((6,)),
            pltpu.SemaphoreType.DMA((6,)),
        ],
        compiler_params=pltpu.CompilerParams(
            collective_id=1, has_side_effects=True, vmem_limit_bytes=67043328
        ),
        name="layer_part",
    )(
        expert_input,
        grad_out,
        routes,
        up,
        down,
        out_weight,
        value,
        in_basis,
        out_basis,
        taps,
        step,
        decay,
        skip[None],
    )


def results_kernel(*refs):
    sources, targets, held, (in_sem, out_sem) = refs[0:4], refs[4:8], refs[8:12], refs[12:14]
    loads, stores = [], []
    for place in range(4):
        loads.append(pltpu.make_async_copy(sources[place], held[place], in_sem.at[place]))
        loads[-1].start()
    for place in range(4):
        loads[place].wait()
        stores.append(pltpu.make_async_copy(held[place], targets[place], out_sem.at[place]))
        stores[-1].start()
    for store in stores:
        store.wait()


def results(*arrays):
    shapes = [jax.ShapeDtypeStruct(array.shape, array.dtype) for array in arrays]
    hbm = pl.BlockSpec(memory_space=pl.ANY)
    return pl.pallas_call(
        results_kernel,
        out_shape=tuple(shapes),
        in_specs=[hbm] * len(arrays),
        out_specs=(hbm,) * len(arrays),
        scratch_shapes=[pltpu.VMEM(array.shape, array.dtype) for array in arrays]
        + [pltpu.SemaphoreType.DMA((len(arrays),))] * 2,
        compiler_params=pltpu.CompilerParams(vmem_limit_bytes=60 * 1024 * 1024),
        name="results",
    )(*arrays)


def shards(
    grad_out,
    expert_input,
    expert_index,
    route_weight,
    up_weight,
    down_weight,
    out_weight,
    *mixer_arrays,
):
    arrays = layer_part(
        grad_out,
        expert_input,
        expert_index,
        route_weight,
        up_weight[0],
        down_weight[0],
        out_weight,
        *mixer_arrays,
    )
    return results(*arrays)


def solution(mesh):
    in_specs = (
        P(("seq", "expert"), None),
        P(("seq", "expert"), None),
        P(("seq", "expert"), None),
        P(("seq", "expert"), None),
        P("expert", None, None),
        P("expert", None, None),
        P("expert", None),
        P("seq", "expert"),
        P(None, "expert"),
        P("expert", "seq"),
        P("expert", "seq"),
        P("expert"),
        P("seq", "expert"),
        P("seq", "expert"),
    )
    out_specs = (
        P(("seq", "expert"), None),
        P("seq", "expert"),
        P("seq", "expert"),
        P("seq", "expert"),
    )
    return jax.shard_map(shards, mesh=mesh, in_specs=in_specs, out_specs=out_specs, check_vma=False)
```

time: 130 us -> 118 us (0.908)
  local copies, waits for them, and re-layouts: 7.61 us -> 0.62 us
  Pallas kernels: 119 us -> 115 us
    unnamed x8 -> x0, local copies, waits for them, and re-layouts: 5.61 us -> none
    pallas_call x2, Pallas kernels: 119 us -> 115 us  [the longest x1 112 us: layer_part(): pl.pallas_call(layer_kernel, out_shape=(jax.ShapeDtypeStruct((rows, wide)...]
where the time goes in v2:
time: 118 us; the launch traced here: 117 us
  Pallas kernels  115 us (97%)
    pallas_call x1, Pallas kernels, layer_part(): pl.pallas_call(layer_kernel, out_shape=(jax.ShapeDtypeStruct((rows, wide)...  112 us
    pallas_call x1, Pallas kernels, results(): pl.pallas_call(results_kernel, out_shape=tuple(shapes), in_specs=[hbm] *...  2.59 us

profile of v2, /device:TPU:24, one launch (start us, length us, event | category | flops | bytes accessed | tf_op | source)
XLA Modules:
  0.0 117.1 jit_solution(7906067009803977501)
XLA Ops:
  0.6 0.7 select_reduce_fusion
  1.3 0.6 broadcast_in_dim.26.route_ref
  2.0 112.4 %layer_part.1 = (bf16[128,2048]{1,0:T(8,128)(2,1)}, bf16[1024,512]{1,0:T(8,128)(2,1)}, bf16[1024,128]{1,0:T(8,128)(2,1)}, bf16[1024,128]{1,0:T(8,128)(2,1)}) custom-call(bf16[128,2048]{1,0:T(8,128)(2,1)} %input_ref.1, bf16[128,2048]{1,0:T(8,128)(2,1)} %grad_ref.1, f32[8,8,128]{2,1,0:T(8,128)} %broadcast_in_dim.26.route_ref, bf16[2048,768]{1,0:T(8,128)(2,1)} %bitcast.3, ...), custom_call_target="tpu_custom_call" | custom-call | tf_op jit(solution)/shard_map/layer_part/pallas_call | solution.py:598
  114.4 2.6 %results.1 = (bf16[128,2048]{1,0:T(8,128)(2,1)}, bf16[1024,512]{1,0:T(8,128)(2,1)}, bf16[1024,128]{1,0:T(8,128)(2,1)}, bf16[1024,128]{1,0:T(8,128)(2,1)}) custom-call(bf16[128,2048]{1,0:T(8,128)(2,1)} %get-tuple-element.8.refs_0_, bf16[1024,512]{1,0:T(8,128)(2,1)} %get-tuple-element.9.refs_1_, bf16[1024,128]{1,0:T(8,128)(2,1)} %get-tuple-element.10.refs_2_, ...), custom_call_target="tpu_custom_call" | custom-call | tf_op jit(solution)/shard_map/results/pallas_call | solution.py:698

commit v3 on v2

--- a/solution.py
+++ b/solution.py
@@ -410,6 +410,21 @@
         partial[slot] = dot(inner, up[...], 1, 1).astype(BF16)
         send("p%d" % slot, partial.at[slot, other], sibling_part.at[slot], sibling)
 
+    def after_half(slot, part, other_part, tag):
+        column = jnp.concatenate(
+            [routes[2 * slot].T[part.start : part.start + half, 0:1]]
+            + [routes[2 * slot + 1].T[part.start : part.start + half, 0:1]],
+            axis=0,
+        )
+        both_grads = jnp.concatenate([grads[slot, part], grads[slot, other_part]], axis=0)
+        both_hidden = jnp.concatenate([hidden[slot, part], hidden[slot, other_part]], axis=0)
+        back = dot(both_grads, down[...], 1, 1) * column
+        inner = (both_hidden * back).astype(BF16)
+        product = dot(inner, up[...], 1, 1).astype(BF16)
+        partial[slot, part] = product[0:half]
+        partial[slot, other_part] = product[half : 2 * half]
+        send(tag, partial.at[slot, other_part], sibling_part.at[slot, part], sibling)
+
     loads[0].wait()
     loads[1].wait()
     arrived("xs0")
@@ -458,6 +473,10 @@
     before(1)
     arrived("xs2", "xs4")
     before(2)
+    arrived("gs1")
+    after_half(1, low, other_low, "p1low")
+    arrived("gs2")
+    after_half(2, high, other_high, "p2high")
     share_far("x", inputs)
     arrived("xs5", "xs6")
     before(3)
@@ -466,29 +485,29 @@
     share_far("g", grads)
     arrived("gs5", "gs6")
     after(3)
-    share_near("g", grads)
     arrived("p3")
     summed[0] = partial[3, whole] + sibling_part[3]
     send("fr", summed.at[0, low], far_part.at[0], right)
     send("fl", summed.at[0, high], far_part.at[1], left)
-    arrived("gs2", "gs4")
-    after(2)
-    arrived("gs1", "gs3")
-    after(1)
-    arrived("p2")
+    arrived("p2high")
     summed[1, high] = partial[2, high] + sibling_part[2, high]
     send("nr1", summed.at[1, high], near_part.at[0, high], right)
-    arrived("p1")
+    arrived("p1low")
     summed[2, low] = partial[1, low] + sibling_part[1, low]
     send("nl1", summed.at[2, low], near_part.at[1, low], left)
+    share_near("g", grads)
+    arrived("gs4")
+    after_half(2, low, other_low, "p2low")
+    arrived("gs3")
+    after_half(1, high, other_high, "p1high")
 
     def three(a, b, c):
         return (a.astype(F32) + b.astype(F32) + c.astype(F32)).astype(BF16)
 
-    arrived("fr")
+    arrived("fr", "p2low")
     summed[1, low] = three(partial[2, low], sibling_part[2, low], far_part[0])
     send("nr2", summed.at[1, low], near_part.at[0, low], right)
-    arrived("fl")
+    arrived("fl", "p1high")
     summed[2, high] = three(partial[1, high], sibling_part[1, high], far_part[1])
     send("nl2", summed.at[2, high], near_part.at[1, high], left)
     loads[5].wait()
@@ -503,11 +522,14 @@
             + near_part[1, part].astype(F32)
         ).astype(BF16)
 
-    arrived("nr1", "nl1", "nr2", "nl2")
+    own = gathered.at[0, whole]
+    arrived("nl1", "nr2")
     finish(low)
+    send("or1", own.at[low], gathered.at[1, low], right)
+    arrived("nr1", "nl2")
     finish(high)
-    own = gathered.at[0, whole]
-    first("o", own, gathered)
+    send("ol1", own.at[high], gathered.at[2, high], left)
+    send("os0", own, gathered.at[0, other], sibling)
     second("o", own, gathered)
     store = pltpu.make_async_copy(own, residual_ref, local_sem.at[0])
     store.start()

time: 118 us -> 117 us (level)
  Pallas kernels: 115 us -> 113 us
    pallas_call x1, Pallas kernels: 112 us -> 111 us  [layer_part(): pl.pallas_call(layer_kernel, out_shape=(jax.ShapeDtypeStruct((rows, wide)...]
where the time goes in v3:
time: 117 us; the launch traced here: 115 us
  Pallas kernels  113 us (97%)
    pallas_call x1, Pallas kernels, layer_part(): pl.pallas_call(layer_kernel, out_shape=(jax.ShapeDtypeStruct((rows, wide)...  111 us
    pallas_call x1, Pallas kernels, results(): pl.pallas_call(results_kernel, out_shape=tuple(shapes), in_specs=[hbm] *...  2.59 us

profile of v3, /device:TPU:24, one launch (start us, length us, event | category | flops | bytes accessed | tf_op | source)
XLA Modules:
  0.0 115.5 jit_solution(3705185275479436080)
XLA Ops:
  0.6 0.7 select_reduce_fusion
  1.3 0.6 broadcast_in_dim.26.route_ref
  2.0 110.7 %layer_part.1 = (bf16[128,2048]{1,0:T(8,128)(2,1)}, bf16[1024,512]{1,0:T(8,128)(2,1)}, bf16[1024,128]{1,0:T(8,128)(2,1)}, bf16[1024,128]{1,0:T(8,128)(2,1)}) custom-call(bf16[128,2048]{1,0:T(8,128)(2,1)} %input_ref.1, bf16[128,2048]{1,0:T(8,128)(2,1)} %grad_ref.1, f32[8,8,128]{2,1,0:T(8,128)} %broadcast_in_dim.26.route_ref, bf16[2048,768]{1,0:T(8,128)(2,1)} %bitcast.3, ...), custom_call_target="tpu_custom_call" | custom-call | tf_op jit(solution)/shard_map/layer_part/pallas_call | solution.py:620
  112.7 2.6 %results.1 = (bf16[128,2048]{1,0:T(8,128)(2,1)}, bf16[1024,512]{1,0:T(8,128)(2,1)}, bf16[1024,128]{1,0:T(8,128)(2,1)}, bf16[1024,128]{1,0:T(8,128)(2,1)}) custom-call(bf16[128,2048]{1,0:T(8,128)(2,1)} %get-tuple-element.8.refs_0_, bf16[1024,512]{1,0:T(8,128)(2,1)} %get-tuple-element.9.refs_1_, bf16[1024,128]{1,0:T(8,128)(2,1)} %get-tuple-element.10.refs_2_, ...), custom_call_target="tpu_custom_call" | custom-call | tf_op jit(solution)/shard_map/results/pallas_call | solution.py:720
